TPU v7x, 32 devices: a whole 2x2x4 slice. The times are simulated.
32 devices in a mesh: dom: 2 (over y), dp: 16 (over z, x, core).
Axes of the slice: x: 2, y: 2, z: 4, core: 2. Of those that a mesh axis runs over, the one named last changes fastest.
Arguments:
- positions: float32 [1024, 128], P(('dom', 'dp')), may hold values from -6 to 6
- length_scale: float32 [1], replicated, may hold values from 16 to 128
- features: float32 [32768, 128], P('dp'), may hold values from -0.5 to 0.5
- labels: int32 [32768], P('dp'), may hold values 0 or 1
- batch_index: int32 [8192], P('dp'), may hold values from 0 to 2047
Outputs:
- moved: float32 [1024, 128], P(('dom', 'dp'))
- score: float32 [1024, 128], P(('dom', 'dp'))
Inputs may be any that keep to these rules, and one draw needn't show every extreme that they name: `batch_index`: an index into the 2048 feature rows of the same dp index.
All inputs are finite; a program needn't handle non-finite values. No bound on the sum of `labels` on one device may be relied on, other than what follows from the above.
Results may differ from a plain program's by a relative error of at most 0.0001.
Values sent between devices are 32-bit elements; how exact they have to be, the bound alone decides.
No kernel may reach another device: no remote copies, remote signals or barrier semaphores. Data moves between devices by JAX's collectives and lax.ppermute only.
A program may use at most 64 MiB of HBM per device.

v0:
```python
import math

import jax
import jax.numpy as jnp
from jax import lax
from jax.sharding import PartitionSpec as P

STEPS = 2


HIGH = lax.Precision.HIGHEST
STEP_SIZE = 2.0


def likelihood(block, rows, targets, scale):
    logits = jnp.dot(block, rows.T, precision=HIGH, preferred_element_type=jnp.float32)
    resid = targets[None, :] - jax.nn.sigmoid(logits)
    return jnp.dot(resid, rows, precision=HIGH, preferred_element_type=jnp.float32) * scale


def displace(aimed, sources, source_score, spread):
    square_a = jnp.sum(aimed * aimed, axis=1)
    square_b = jnp.sum(sources * sources, axis=1)
    inner = jnp.dot(aimed, sources.T, precision=HIGH, preferred_element_type=jnp.float32)
    dist = square_a[:, None] + square_b[None, :] - 2.0 * inner
    kernel = lax.rsqrt(1.0 + dist / spread)
    cubed = kernel * kernel * kernel
    drive = jnp.dot(kernel, source_score, precision=HIGH, preferred_element_type=jnp.float32)
    pulled = jnp.dot(cubed, sources, precision=HIGH, preferred_element_type=jnp.float32)
    return drive + (aimed * jnp.sum(cubed, axis=1)[:, None] - pulled) / spread


def shards(positions, length_scale, features, labels, batch_index):
    rows = features[batch_index]
    targets = labels[batch_index].astype(jnp.float32)
    scale = 1.0 / math.sqrt(batch_index.shape[0] * lax.axis_size("dp"))
    spread = length_scale[0]
    local_count = positions.shape[0]
    particle_total = local_count * lax.axis_size("dom") * lax.axis_size("dp")
    factor = STEP_SIZE / particle_total
    current = positions
    score = positions
    for iteration in range(STEPS):
        block = lax.all_gather(current, "dp", axis=0, tiled=True)
        gradient_block = lax.psum(likelihood(block, rows, targets, scale), "dp")
        score_block = gradient_block - block
        place = lax.axis_index("dp") * local_count
        score = lax.dynamic_slice_in_dim(score_block, place, local_count, 0)
        aimed_all = lax.all_gather(current, "dom", axis=0, tiled=True)
        moves = lax.psum_scatter(
            displace(aimed_all, block, score_block, spread), "dom", scatter_dimension=0, tiled=True
        )
        current = current + factor * moves
    return (current, score)


def solution(mesh):
    placed = (P(("dom", "dp"), None), P(), P("dp", None), P("dp"), P("dp"))
    return jax.shard_map(
        shards,
        mesh=mesh,
        in_specs=placed,
        out_specs=(P(("dom", "dp"), None), P(("dom", "dp"), None)),
        check_vma=False,
    )
```

profile of v0, /device:TPU:0, one launch (start us, length us, event | category | flops | bytes accessed | tf_op | source)
XLA Modules:
  0.0 272.5 jit_solution(17130246005774058776)
XLA Ops:
  7.2 0.0 copy-start
  7.2 0.0 copy-start.3
  7.2 0.0 all-reduce.3.cloned.1.call-start
  7.2 24.2 %all_gather.13 = f32[512,128]{1,0:T(8,128)S(1)} all-gather(f32[32,128]{1,0:T(8,128)} %param.5), channel_id=1, replica_groups=mesh['dom'=2,'dp'=16] {'dp'}, dimensions={0}, use_global_device_ids=true | all-gather | bytes 278528 | tf_op jit(solution)/shard_map/all_gather | solution.py:44
  31.4 0.0 copy-done.3
  31.4 0.0 copy-done
  31.4 0.0 copy-start.1
  31.5 1.0 gather_fusion.1
  32.5 0.0 copy-done.1
  32.5 3.1 %gather_fusion = s32[512]{0:T(512)S(1)} fusion(s32[2048]{0:T(1024)S(1)} %copy-done.1, s32[1024]{0:T(1024)S(1)} %pad_clamp_fusion), kind=kCustom, calls=%fused_computation | custom fusion | bytes 6144 | tf_op jit(solution)/shard_map/gather | solution.py:35
  35.7 1.1 fusion.4
  36.8 2.5 convolution_multiply_fusion.1
  39.4 0.0 all-reduce.3.cloned.1.call-update
  39.4 0.0 copy-start.2
  39.4 0.0 reduce-scatter.3.cloned.1.call-start
  39.4 0.1 multiply_reduce_fusion.1
  39.6 0.5 copy-done.2
  40.1 4.4 %all_gather.12 = f32[64,128]{1,0:T(8,128)S(1)} all-gather(f32[32,128]{1,0:T(8,128)S(1)} %copy-done.2), channel_id=1, replica_groups=mesh['dom'=2,'dp'=16] {'dom'}, dimensions={0}, use_global_device_ids=true | all-gather | bytes 49152 | tf_op jit(solution)/shard_map/all_gather | solution.py:49
  45.1 0.1 multiply_reduce_fusion.3
  45.3 0.5 fusion.22
  45.8 80.9 %all-reduce.3.cloned.1.call-done = f32[512,128]{1,0:T(8,128)} async-done(((f32[512,128]{1,0:T(8,128)}), f32[512,128]{1,0:T(8,128)}) %all-reduce.3.cloned.1.call-update) | async-done | bytes 262160 | tf_op jit(solution)/shard_map/psum | solution.py:45
  126.6 1.2 fusion.20
  127.9 0.9 fusion.19
  128.8 0.0 reduce-scatter.3.cloned.1.call-update
  128.8 0.0 all-reduce.5.cloned.1.call-start
  128.8 10.6 %reduce-scatter.3.cloned.1.call-done = f32[32,128]{1,0:T(8,128)} async-done(((f32[64,128]{1,0:T(8,128)}), f32[32,128]{1,0:T(8,128)}) %reduce-scatter.3.cloned.1.call-update) | async-done | bytes 16400 | tf_op jit(solution)/shard_map/reduce_scatter | solution.py:50
  139.4 0.7 multiply_add_fusion.1
  140.1 22.0 %all_gather.15 = f32[512,128]{1,0:T(8,128)S(1)} all-gather(f32[32,128]{1,0:T(8,128)S(1)} %multiply_add_fusion.1), channel_id=1, replica_groups=mesh['dom'=2,'dp'=16] {'dp'}, dimensions={0}, use_global_device_ids=true | all-gather | bytes 278528 | tf_op jit(solution)/shard_map/all_gather | solution.py:44
  162.1 1.1 fusion.7
  163.3 1.7 convolution_multiply_fusion
  165.0 0.0 all-reduce.5.cloned.1.call-update
  165.0 0.0 reduce-scatter.5.cloned.1.call-start
  165.0 4.4 %all_gather.14 = f32[64,128]{1,0:T(8,128)S(1)} all-gather(f32[32,128]{1,0:T(8,128)S(1)} %multiply_add_fusion.1), channel_id=1, replica_groups=mesh['dom'=2,'dp'=16] {'dom'}, dimensions={0}, use_global_device_ids=true | all-gather | bytes 49152 | tf_op jit(solution)/shard_map/all_gather | solution.py:49
  169.4 0.1 multiply_reduce_fusion.2
  169.5 81.7 %all-reduce.5.cloned.1.call-done = f32[512,128]{1,0:T(8,128)} async-done(((f32[512,128]{1,0:T(8,128)}), f32[512,128]{1,0:T(8,128)}) %all-reduce.5.cloned.1.call-update) | async-done | bytes 262160 | tf_op jit(solution)/shard_map/psum | solution.py:45
  251.2 1.1 fusion.24
  252.3 0.5 fusion.23
  252.8 0.3 fusion.25
  253.1 0.9 fusion.17
  254.0 0.0 reduce-scatter.5.cloned.1.call-update
  254.1 0.6 constant_dynamic-slice_fusion
  254.7 10.0 %reduce-scatter.5.cloned.1.call-done = f32[32,128]{1,0:T(8,128)} async-done(((f32[64,128]{1,0:T(8,128)}), f32[32,128]{1,0:T(8,128)}) %reduce-scatter.5.cloned.1.call-update) | async-done | bytes 16400 | tf_op jit(solution)/shard_map/reduce_scatter | solution.py:50
  264.7 1.3 multiply_add_fusion
  (3 shorter events, 0.0 us)
Async XLA Ops:
  7.2 24.3 %copy-start = (f32[2048,128]{1,0:T(8,128)S(1)}, f32[2048,128]{1,0:T(8,128)}, u32[]{:S(2)}) copy-start(f32[2048,128]{1,0:T(8,128)} %param.7) | copy-start | bytes 3145732
  7.2 24.2 %copy-start.3 = (s32[512]{0:T(512)S(1)}, s32[512]{0:T(512)}, u32[]{:S(2)}) copy-start(s32[512]{0:T(512)} %param.9) | copy-start | bytes 6148
  7.2 119.4 %all-reduce.3.cloned.1.call-start = ((), (), s32[]{:S(2)}) async-start(), calls=%async_computation.2 | async-start | bytes 524288 | tf_op jit(solution)/shard_map/psum | solution.py:45
  31.4 1.1 copy-start.1
  39.4 0.7 copy-start.2
  39.4 100.0 %reduce-scatter.3.cloned.1.call-start = ((), (), s32[]{:S(2)}) async-start(), calls=%async_computation.3 | async-start | bytes 49152 | tf_op jit(solution)/shard_map/reduce_scatter | solution.py:50
  128.8 122.4 %all-reduce.5.cloned.1.call-start = ((), (), s32[]{:S(2)}) async-start(), calls=%async_computation.4 | async-start | bytes 524288 | tf_op jit(solution)/shard_map/psum | solution.py:45
  165.0 99.7 %reduce-scatter.5.cloned.1.call-start = ((), (), s32[]{:S(2)}) async-start(), calls=%async_computation.5 | async-start | bytes 49152 | tf_op jit(solution)/shard_map/reduce_scatter | solution.py:50
Sparse Core Ops, SparseCore 0:
  39.5 87.0 all-reduce.2
  128.9 10.4 reduce-scatter.2
  165.1 86.0 all-reduce.4
  254.2 10.4 reduce-scatter.4
where the time goes:
time: 273 us
  waiting for transfers between devices  183 us (67%)
  blocking collectives  55 us (20%)
  between operations  14.5 us (5%)
  matrix products  10.8 us (4%)
  local copies, waits for them, and re-layouts  5.33 us (2%)
  other arithmetic  3.51 us (1%)
    psum x2, waiting for transfers between devices, shards(): gradient_block = lax.psum(likelihood(block, rows, targets, scale), 'dp')  163 us
    all_gather x2, blocking collectives, shards(): block = lax.all_gather(current, 'dp', axis=0, tiled=True)  46.2 us
    reduce_scatter x2, waiting for transfers between devices, shards(): lax.psum_scatter(displace(aimed_all, block, score_block, spread), 'dom',...  20.6 us
    all_gather x2, blocking collectives, shards(): aimed_all = lax.all_gather(current, 'dom', axis=0, tiled=True)  8.8 us
  transfers between devices with their start and end apart: 4, of which 4 were waited for; matrix products, arithmetic and copies ran while one was open for 1% of the time, Pallas kernels for 0%

commit v1 on v0

v1 whole, which is shorter than its diff:
```python
import math

import jax
import jax.numpy as jnp
from jax import lax
from jax.sharding import Mesh, PartitionSpec as P

STEPS = 2
STEP_SIZE = 2.0
HIGH = lax.Precision.HIGHEST


def dot(a, b):
    return jnp.dot(a, b, precision=HIGH, preferred_element_type=jnp.float32)


def dot_t(a, b):
    return lax.dot_general(a, b, (((1,), (1,)), ((), ())), precision=HIGH, preferred_element_type=jnp.float32)


def likelihood(block, rows, targets, scale):
    resid = targets[None, :] - jax.nn.sigmoid(dot_t(block, rows))
    return dot(resid, rows) * scale


def inverse_root(aimed, sources, spread):
    square_a = jnp.sum(aimed * aimed, axis=1)
    square_b = jnp.sum(sources * sources, axis=1)
    dist = square_a[:, None] + square_b[None, :] - 2.0 * dot_t(aimed, sources)
    return lax.rsqrt(1.0 + dist / spread)


def partial_move(aimed, sources, grads, own, spread):
    drive = dot(inverse_root(aimed, sources, spread), grads)
    kernel = inverse_root(aimed, own, spread)
    cubed = kernel * kernel * kernel
    pulled = dot(cubed, own)
    return drive - dot(kernel, own) + (aimed * jnp.sum(cubed, axis=1)[:, None] - pulled) / spread


def shifted(x, axis, offset):
    size = lax.axis_size(axis)
    return lax.ppermute(x, axis, [(i, (i + offset) % size) for i in range(size)])


def spread_over(x, axes):
    size = lax.axis_size(axes)
    tiled = jnp.broadcast_to(x[None], (size,) + x.shape)
    return lax.all_to_all(tiled, axes, 0, 0, tiled=True)


def summed_over(x, axes):
    return jnp.sum(lax.all_to_all(x, axes, 0, 0, tiled=True), axis=0)


def shards(positions, length_scale, features, labels, batch_index):
    doms, chips, cores = lax.axis_size("dom"), lax.axis_size("chip"), lax.axis_size("core")
    local, width = positions.shape
    total = local * doms * chips * cores
    scale = 1.0 / math.sqrt(batch_index.shape[0] * chips * cores)
    factor = STEP_SIZE / total
    spread = length_scale[0]
    dom, chip = lax.axis_index("dom"), lax.axis_index("chip")

    def all_cores(x):
        return [x] + [shifted(x, "core", o) for o in range(1, cores)]

    def all_doms(x):
        return [x] + [shifted(x, "dom", o) for o in range(1, doms)]

    rows = jnp.concatenate(all_cores(features[batch_index]), 0)
    targets = jnp.concatenate(all_cores(labels[batch_index].astype(jnp.float32)), 0)

    def flat(blocks):
        return jnp.concatenate([b.reshape(-1, width) for b in blocks], 0)

    def own_of(blocks):
        return flat([lax.dynamic_index_in_dim(b, chip, 0) for b in blocks])

    current = positions
    for iteration in range(STEPS):
        last = iteration == STEPS - 1
        near = spread_over(current, "chip")
        by_dom = all_doms(near)
        if last:
            aimed = near
            graded = by_dom
        else:
            aimed = jnp.roll(jnp.stack(by_dom[:1] + by_dom[:0:-1]), dom, axis=0)
            graded = [near]
        grads = [likelihood(b.reshape(-1, width), rows, targets, scale) for b in graded]
        sources = [s for b in graded for s in all_cores(b)]
        source_grads = [s for g in grads for s in all_cores(g)]
        moves = partial_move(aimed.reshape(-1, width), flat(sources), flat(source_grads), own_of(sources), spread)
        if last:
            both = jnp.concatenate([moves.reshape(chips, local, width), grads[0].reshape(chips, local, width)], 1)
            result = summed_over(both, "chip")
            score = result[local:] - current
            current = current + factor * result[:local]
        else:
            moves = summed_over(moves.reshape(doms * chips, local, width), ("dom", "chip"))
            current = current + factor * moves
    return (current, score)


def solution(mesh):
    doms, dp = mesh.shape["dom"], mesh.shape["dp"]
    cores = 2 if dp % 2 == 0 else 1
    inner = Mesh(mesh.devices.reshape(doms, dp // cores, cores), ("dom", "chip", "core"))
    dp_axes = ("chip", "core")
    placed = (P(("dom",) + dp_axes, None), P(), P(dp_axes, None), P(dp_axes), P(dp_axes))
    return jax.shard_map(
        shards,
        mesh=inner,
        in_specs=placed,
        out_specs=(P(("dom",) + dp_axes, None), P(("dom",) + dp_axes, None)),
        check_vma=False,
    )
```

time: 273 us -> 80.6 us (0.30)
  waiting for transfers between devices: 183 us -> 6.49 us
  blocking collectives: 55 us -> 38 us
  between operations: 14.5 us -> 1.62 us
  starting transfers between devices: 0.16 us -> 11.8 us
  matrix products: 10.8 us -> 14.1 us
    psum x2 -> x0, waiting for transfers between devices: 163 us -> none  [shards(): gradient_block = lax.psum(likelihood(block, rows, targets, scale), 'dp')]
    all_gather x4 -> x0, blocking collectives: 55 us -> none  [the longest x2 46.2 us: shards(): block = lax.all_gather(current, 'dp', axis=0, tiled=True)]
    all_to_all x0 -> x3, blocking collectives: none -> 38 us  [the longest x2 27.6 us: summed_over(): return jnp.sum(lax.all_to_all(x, axes, 0, 0, tiled=True), axis=0)]
    reduce_scatter x2 -> x0, waiting for transfers between devices: 20.6 us -> none  [shards(): lax.psum_scatter(displace(aimed_all, block, score_block, spread), 'dom',...]
    all_to_all x0 -> x1, starting transfers between devices: none -> 7.41 us  [spread_over(): return lax.all_to_all(tiled, axes, 0, 0, tiled=True)]
    ppermute x0 -> x10, waiting for transfers between devices: none -> 4.87 us  [shifted(): lax.ppermute(x, axis, [(i, (i + offset) % size) for i in range(size)])]
    ppermute x0 -> x10, starting transfers between devices: none -> 4.4 us  [shifted(): lax.ppermute(x, axis, [(i, (i + offset) % size) for i in range(size)])]
    dot_general x10 -> x16, matrix products: 10.8 us -> 14.1 us  [the longest x9 7.65 us: dot(): return jnp.dot(a, b, precision=HIGH, preferred_element_type=jnp.float32)]
  transfers between devices with their start and end apart: 4 -> 11, of which waited for: 4 -> 4; matrix products, arithmetic and copies ran while one was open for 1% -> 19% of each run, Pallas kernels for 0% -> 0%
where the time goes in v1:
time: 80.6 us; the launch traced here: 80.1 us
  blocking collectives  38 us (47%)
  matrix products  14.1 us (17%)
  starting transfers between devices  11.8 us (15%)
  local copies, waits for them, and re-layouts  6.58 us (8%)
  waiting for transfers between devices  6.49 us (8%)
  between operations  1.62 us (2%)
  other arithmetic  1.52 us (2%)
    all_to_all x2, blocking collectives, summed_over(): return jnp.sum(lax.all_to_all(x, axes, 0, 0, tiled=True), axis=0)  27.6 us
    all_to_all x1, blocking collectives, spread_over(): return lax.all_to_all(tiled, axes, 0, 0, tiled=True)  10.4 us
    dot_general x9, matrix products, dot(): return jnp.dot(a, b, precision=HIGH, preferred_element_type=jnp.float32)  7.65 us
    all_to_all x1, starting transfers between devices, spread_over(): return lax.all_to_all(tiled, axes, 0, 0, tiled=True)  7.41 us
    dot_general x7, matrix products, dot_t(): lax.dot_general(a, b, (((1,), (1,)), ((), ())), precision=HIGH, preferred...  6.43 us
    ppermute x10, waiting for transfers between devices, shifted(): lax.ppermute(x, axis, [(i, (i + offset) % size) for i in range(size)])  4.87 us
    ppermute x10, starting transfers between devices, shifted(): lax.ppermute(x, axis, [(i, (i + offset) % size) for i in range(size)])  4.4 us
    gather x1, local copies, waits for them, and re-layouts, shards(): labels[batch_index].astype(jnp.float32)  3.14 us
  transfers between devices with their start and end apart: 11, of which 4 were waited for; matrix products, arithmetic and copies ran while one was open for 19% of the time, Pallas kernels for 0%

profile of v1, /device:TPU:0, one launch (start us, length us, event | category | flops | bytes accessed | tf_op | source)
XLA Modules:
  0.0 80.1 jit_solution(1681161565108543829)
XLA Ops:
  0.6 0.0 copy-start
  0.6 1.5 %broadcast_in_dim.6 = f32[8,32,128]{2,1,0:T(8,128)} broadcast(f32[32,128]{1,0:T(8,128)} %param.5), dimensions={1,2} | broadcast | bytes 147456 | tf_op jit(solution)/shard_map/broadcast_in_dim | solution.py:48
  2.1 7.4 %all-to-all-start = ((f32[8,32,128]{2,1,0:T(8,128)}), f32[8,32,128]{2,1,0:T(8,128)S(1)}, u32[]{:S(2)}, u32[]{:S(2)}) async-start(f32[8,32,128]{2,1,0:T(8,128)} %broadcast_in_dim.6), calls=%async_computation | async-start | bytes 262144 | tf_op jit(solution)/shard_map/all_to_all | solution.py:49
  9.6 0.0 copy-start.1
  9.6 1.0 %gather_fusion.1 = f32[512,128]{1,0:T(8,128)S(1)} fusion(f32[2048,128]{1,0:T(8,128)S(1)} %copy-done, s32[1024]{0:T(1024)S(1)} %pad_clamp_fusion), kind=kCustom, calls=%fused_computation.1 | custom fusion | bytes 526336 | tf_op jit(solution)/shard_map/gather | solution.py:71
  10.6 0.1 collective-permute-start.3
  10.7 3.1 %gather_fusion = s32[512]{0:T(512)S(1)} fusion(s32[2048]{0:T(1024)S(1)} %copy-done.1, s32[1024]{0:T(1024)S(1)} %pad_clamp_fusion), kind=kCustom, calls=%fused_computation | custom fusion | bytes 6144 | tf_op jit(solution)/shard_map/gather | solution.py:72
  13.9 0.5 collective-permute-start.2
  15.1 0.1 collective-permute-done.2
  15.2 1.6 %all-to-all-done = f32[8,32,128]{2,1,0:T(8,128)S(1)} async-done(((f32[8,32,128]{2,1,0:T(8,128)}), f32[8,32,128]{2,1,0:T(8,128)S(1)}, u32[]{:S(2)}, u32[]{:S(2)}) %all-to-all-start) | async-done | bytes 131104 | tf_op jit(solution)/shard_map/all_to_all | solution.py:49
  16.9 1.5 %collective-permute-start = (f32[8,32,128]{2,1,0:T(8,128)S(1)}, f32[8,32,128]{2,1,0:T(8,128)S(1)}, u32[]{:S(2)}, u32[]{:S(2)}) collective-permute-start(f32[8,32,128]{2,1,0:T(8,128)S(1)} %all-to-all-done), channel_id=1, source_target_pairs={{0,16},{16,0},{1,17},{17,1},{2,18},{18,2},{3,19},{19,3},{4,20},{20... | collective-permute-start | bytes 393224 | tf_op jit(solution)/shard_map/ppermute | solution.py:43
  18.4 1.0 %fusion.14 = f32[1024,256]{1,0:T(8,128)S(1)} fusion(f32[1024,128]{1,0:T(8,128)S(1)} %constant_dynamic-update-slice_fusion, f32[256,128]{1,0:T(8,128)S(1)} %bitcast.50), kind=kOutput, calls=%fused_computation.20 | convolution fusion | flops 403439616 | bytes 1703936 | tf_op jit(solution)/shard_map/dot_general | solution.py:18
  19.4 2.0 %convolution_multiply_fusion.6 = f32[256,128]{1,0:T(8,128)S(1)} fusion(f32[1024,128]{1,0:T(8,128)S(1)} %constant_dynamic-update-slice_fusion, f32[1024,256]{1,0:T(8,128)S(1)} %fusion.14, f32[1024]{0:T(1024)S(1)} %pad_maximum_fusion.10), kind=kOutput, calls=%fused_computation.46 | convolution fusion | flops 402948096 | bytes 1708032 | tf_op jit(solution)/shard_map/dot_general | solution.py:14
  21.4 0.6 collective-permute-start.4
  22.0 0.2 multiply_reduce_fusion.2
  22.1 0.1 add.124
  22.2 0.1 multiply_reduce_fusion.1
  22.4 0.1 multiply_reduce_fusion.5
  22.5 0.5 fusion.47
  22.9 1.1 %fusion.18 = f32[512,512]{1,0:T(8,128)S(1)} fusion(f32[512,128]{1,0:T(8,128)S(1)} %bitcast.63, f32[]{:T(128)} %bitcast.44, f32[512]{0:T(512)S(1)} %multiply_reduce_fusion.1, f32[512]{0:T(512)S(1)} %add.124, f32[256,128]{1,0:T(8,128)S(1)} %bitcast.66, f32[256,128]{1,0:T(8,128)S(1)} %bitcast.53), kind=kOutput, calls=%fused_computation.25 | convolution fusion | flops 404029440 | bytes 1576964 | tf_op jit(solution)/shard_map/dot_general | solution.py:18
  24.1 0.6 fusion.19
  24.7 0.6 fusion.50
  25.3 1.0 %fusion.20 = f32[512,128]{1,0:T(8,128)S(1)} fusion(f32[512,128]{1,0:T(8,128)S(1)} %fusion.19, f32[512,128]{1,0:T(8,128)S(1)} %fusion.50, f32[512,512]{1,0:T(8,128)S(1)} %fusion.18, f32[256,128]{1,0:T(8,128)S(1)} %collective-permute-done.4, f32[256,128]{1,0:T(8,128)S(1)} %convolution_multiply_fusion.6), kind=kOutput, calls=%fused_computation.29 | convolution fusion | flops 402849792 | bytes 2097152 | tf_op jit(solution)/shard_map/dot_general | solution.py:14
  26.3 15.5 %all_to_all.20 = f32[16,32,128]{2,1,0:T(8,128)S(1)} all-to-all(f32[16,32,128]{2,1,0:T(8,128)S(1)} %bitcast.60), channel_id=1, replica_groups=mesh['dom'=2,'chip'=8,'core'=2] {'dom','chip'}, dimensions={0} | all-to-all | bytes 524288 | tf_op jit(solution)/shard_map/all_to_all | solution.py:53
  41.8 0.7 copy-done.2
  42.5 10.4 %all_to_all.21 = f32[8,32,128]{2,1,0:T(8,128)S(1)} all-to-all(f32[8,32,128]{2,1,0:T(8,128)S(1)} %broadcast_in_dim.8), channel_id=1, replica_groups=mesh['dom'=2,'chip'=8,'core'=2] {'chip'}, dimensions={0} | all-to-all | bytes 262144 | tf_op jit(solution)/shard_map/all_to_all | solution.py:49
  52.9 1.1 %fusion.7 = f32[256,1024]{1,0:T(8,128)S(1)} fusion(f32[256,128]{1,0:T(8,128)S(1)} %bitcast.54, f32[1024,128]{1,0:T(8,128)S(1)} %constant_dynamic-update-slice_fusion, f32[1024]{0:T(1024)S(1)} %pad_maximum_fusion.10), kind=kOutput, calls=%fused_computation.11 | convolution fusion | flops 403701760 | bytes 1708032 | tf_op jit(solution)/shard_map/dot_general | solution.py:18
  54.1 1.0 %convolution_multiply_fusion.4 = f32[256,128]{1,0:T(8,128)S(1)} fusion(f32[256,1024]{1,0:T(8,128)S(1)} %fusion.7, f32[1024,128]{1,0:T(8,128)S(1)} %constant_dynamic-update-slice_fusion), kind=kOutput, calls=%fused_computation.40 | convolution fusion | flops 402685952 | bytes 1703936 | tf_op jit(solution)/shard_map/dot_general | solution.py:14
  55.1 0.6 collective-permute-start.6
  55.7 0.1 multiply_reduce_fusion.3
  55.8 0.1 add.140
  55.9 0.0 collective-permute-start.8
  55.9 0.5 collective-permute-start.5
  56.4 3.7 %collective-permute-done.6 = f32[8,32,128]{2,1,0:T(8,128)S(1)} collective-permute-done((f32[8,32,128]{2,1,0:T(8,128)S(1)}, f32[8,32,128]{2,1,0:T(8,128)S(1)}, u32[]{:S(2)}, u32[]{:S(2)}) %collective-permute-start.6) | collective-permute-done | bytes 131104 | tf_op jit(solution)/shard_map/ppermute | solution.py:43
  60.1 1.1 %fusion.3 = f32[256,1024]{1,0:T(8,128)S(1)} fusion(f32[256,128]{1,0:T(8,128)S(1)} %bitcast.67, f32[1024,128]{1,0:T(8,128)S(1)} %constant_dynamic-update-slice_fusion, f32[1024]{0:T(1024)S(1)} %pad_maximum_fusion.10), kind=kOutput, calls=%fused_computation.6 | convolution fusion | flops 403701760 | bytes 1708032 | tf_op jit(solution)/shard_map/dot_general | solution.py:18
  61.2 1.0 %convolution_multiply_fusion.3 = f32[256,128]{1,0:T(8,128)S(1)} fusion(f32[256,1024]{1,0:T(8,128)S(1)} %fusion.3, f32[1024,128]{1,0:T(8,128)S(1)} %constant_dynamic-update-slice_fusion), kind=kOutput, calls=%fused_computation.39 | convolution fusion | flops 402685952 | bytes 1703936 | tf_op jit(solution)/shard_map/dot_general | solution.py:14
  62.2 0.1 collective-permute-start.9
  62.3 0.5 collective-permute-start.7
  62.8 1.0 %collective-permute-done.7 = f32[8,32,128]{2,1,0:T(8,128)S(1)} collective-permute-done((f32[8,32,128]{2,1,0:T(8,128)S(1)}, f32[8,32,128]{2,1,0:T(8,128)S(1)}, u32[]{:S(2)}, u32[]{:S(2)}) %collective-permute-start.7) | collective-permute-done | bytes 131104 | tf_op jit(solution)/shard_map/ppermute | solution.py:43
  63.8 0.2 multiply_reduce_fusion
  64.1 0.1 multiply_reduce_fusion.4
  64.2 0.4 fusion.48
  64.6 1.1 %fusion.11 = f32[256,1024]{1,0:T(8,128)S(1)} fusion(f32[256,128]{1,0:T(8,128)S(1)} %bitcast.57, f32[]{:T(128)} %bitcast.47, f32[1024]{0:T(1024)S(1)} %multiply_reduce_fusion, f32[256]{0:T(256)S(1)} %add.140, f32[256,128]{1,0:T(8,128)S(1)} %bitcast.73, f32[256,128]{1,0:T(8,128)S(1)} %bitcast.69, f32[256,128]{1,0:T(8,128)S(1)} %bitcast.71), kind=kOutput, calls=%fused_computation.16 | convolution fusion | flops 404357120 | bytes 1577988 | tf_op jit(solution)/shard_map/dot_general | solution.py:18
  65.7 0.3 fusion.26
  66.0 1.0 %fusion.32 = f32[256,128]{1,0:T(8,128)S(1)} fusion(f32[256,1024]{1,0:T(8,128)S(1)} %fusion.11, f32[256,128]{1,0:T(8,128)S(1)} %collective-permute-done.9, f32[256,128]{1,0:T(8,128)S(1)} %convolution_multiply_fusion.3, f32[256,128]{1,0:T(8,128)S(1)} %collective-permute-done.8, f32[256,128]{1,0:T(8,128)S(1)} %convolution_multiply_fusion.4), kind=kOutput, calls=%fused_computation.53 | convolution fusion | flops 403046400 | bytes 1703936 | tf_op jit(solution)/shard_map/dot_general | solution.py:14
  67.0 0.3 fusion.25
  67.3 12.1 %all_to_all.22 = f32[8,64,128]{2,1,0:T(8,128)S(1)} all-to-all(f32[8,64,128]{2,1,0:T(8,128)S(1)} %pad_maximum_fusion.3), channel_id=1, replica_groups=mesh['dom'=2,'chip'=8,'core'=2] {'chip'}, dimensions={0} | all-to-all | bytes 524288 | tf_op jit(solution)/shard_map/all_to_all | solution.py:53
  79.4 0.6 slice_subtract_fusion
  (30 shorter events, 0.2 us)
Async XLA Ops:
  0.6 8.9 %copy-start = (f32[2048,128]{1,0:T(8,128)S(1)}, f32[2048,128]{1,0:T(8,128)}, u32[]{:S(2)}) copy-start(f32[2048,128]{1,0:T(8,128)} %param.7) | copy-start | bytes 3145732
  2.1 7.4 %copy-start.3 = (s32[512]{0:T(512)S(1)}, s32[512]{0:T(512)}, u32[]{:S(2)}) copy-start(s32[512]{0:T(512)} %param.9) | copy-start | bytes 6148
  2.1 14.8 %all-to-all-start = ((f32[8,32,128]{2,1,0:T(8,128)}), f32[8,32,128]{2,1,0:T(8,128)S(1)}, u32[]{:S(2)}, u32[]{:S(2)}) async-start(f32[8,32,128]{2,1,0:T(8,128)} %broadcast_in_dim.6), calls=%async_computation | async-start | bytes 262144 | tf_op jit(solution)/shard_map/all_to_all | solution.py:49
  9.6 1.1 %copy-start.1 = (s32[2048]{0:T(1024)S(1)}, s32[2048]{0:T(1024)}, u32[]{:S(2)}) copy-start(s32[2048]{0:T(1024)} %param.8) | copy-start | bytes 24580
  10.6 7.8 %collective-permute-start.3 = (f32[512,128]{1,0:T(8,128)S(1)}, f32[512,128]{1,0:T(8,128)S(1)}, u32[]{:S(2)}, u32[]{:S(2)}) collective-permute-start(f32[512,128]{1,0:T(8,128)S(1)} %gather_fusion.1), channel_id=1, source_target_pairs={{0,1},{1,0},{2,3},{3,2},{4,5},{5,4},{6,7},{7,6},{8,9},{9,8},{10,11... | collective-permute-start | bytes 786440 | tf_op jit(solution)/shard_map/ppermute | solution.py:43
  13.9 1.4 %collective-permute-start.2 = (f32[512]{0:T(512)S(1)}, f32[512]{0:T(512)S(1)}, u32[]{:S(2)}, u32[]{:S(2)}) collective-permute-start(f32[512]{0:T(512)S(1)} %convert_element_type.3), channel_id=1, source_target_pairs={{0,1},{1,0},{2,3},{3,2},{4,5},{5,4},{6,7},{7,6},{8,9},{9,8},{10,11... | collective-permute-start | bytes 6152 | tf_op jit(solution)/shard_map/ppermute | solution.py:43
  16.9 5.1 %collective-permute-start = (f32[8,32,128]{2,1,0:T(8,128)S(1)}, f32[8,32,128]{2,1,0:T(8,128)S(1)}, u32[]{:S(2)}, u32[]{:S(2)}) collective-permute-start(f32[8,32,128]{2,1,0:T(8,128)S(1)} %all-to-all-done), channel_id=1, source_target_pairs={{0,16},{16,0},{1,17},{17,1},{2,18},{18,2},{3,19},{19,3},{4,20},{20... | collective-permute-start | bytes 393224 | tf_op jit(solution)/shard_map/ppermute | solution.py:43
  18.4 3.8 %collective-permute-start.1 = (f32[8,32,128]{2,1,0:T(8,128)S(1)}, f32[8,32,128]{2,1,0:T(8,128)S(1)}, u32[]{:S(2)}, u32[]{:S(2)}) collective-permute-start(f32[8,32,128]{2,1,0:T(8,128)S(1)} %all-to-all-done), channel_id=1, source_target_pairs={{0,1},{1,0},{2,3},{3,2},{4,5},{5,4},{6,7},{7,6},{8,9},{9,8},{10,11... | collective-permute-start | bytes 393224 | tf_op jit(solution)/shard_map/ppermute | solution.py:43
  21.4 3.9 %collective-permute-start.4 = (f32[256,128]{1,0:T(8,128)S(1)}, f32[256,128]{1,0:T(8,128)S(1)}, u32[]{:S(2)}, u32[]{:S(2)}) collective-permute-start(f32[256,128]{1,0:T(8,128)S(1)} %convolution_multiply_fusion.6), channel_id=1, source_target_pairs={{0,1},{1,0},{2,3},{3,2},{4,5},{5,4},{6,7},{7,6},{8,9},{9,8},{10,11... | collective-permute-start | bytes 393224 | tf_op jit(solution)/shard_map/ppermute | solution.py:43
  41.8 0.7 copy-start.2
  55.1 5.0 %collective-permute-start.6 = (f32[8,32,128]{2,1,0:T(8,128)S(1)}, f32[8,32,128]{2,1,0:T(8,128)S(1)}, u32[]{:S(2)}, u32[]{:S(2)}) collective-permute-start(f32[8,32,128]{2,1,0:T(8,128)S(1)} %all_to_all.21), channel_id=1, source_target_pairs={{0,16},{16,0},{1,17},{17,1},{2,18},{18,2},{3,19},{19,3},{4,20},{20... | collective-permute-start | bytes 393224 | tf_op jit(solution)/shard_map/ppermute | solution.py:43
  55.9 10.1 %collective-permute-start.8 = (f32[256,128]{1,0:T(8,128)S(1)}, f32[256,128]{1,0:T(8,128)S(1)}, u32[]{:S(2)}, u32[]{:S(2)}) collective-permute-start(f32[256,128]{1,0:T(8,128)S(1)} %convolution_multiply_fusion.4), channel_id=1, source_target_pairs={{0,1},{1,0},{2,3},{3,2},{4,5},{5,4},{6,7},{7,6},{8,9},{9,8},{10,11... | collective-permute-start | bytes 393224 | tf_op jit(solution)/shard_map/ppermute | solution.py:43
  55.9 6.9 %collective-permute-start.5 = (f32[8,32,128]{2,1,0:T(8,128)S(1)}, f32[8,32,128]{2,1,0:T(8,128)S(1)}, u32[]{:S(2)}, u32[]{:S(2)}) collective-permute-start(f32[8,32,128]{2,1,0:T(8,128)S(1)} %all_to_all.21), channel_id=1, source_target_pairs={{0,1},{1,0},{2,3},{3,2},{4,5},{5,4},{6,7},{7,6},{8,9},{9,8},{10,11... | collective-permute-start | bytes 393224 | tf_op jit(solution)/shard_map/ppermute | solution.py:43
  62.2 3.8 %collective-permute-start.9 = (f32[256,128]{1,0:T(8,128)S(1)}, f32[256,128]{1,0:T(8,128)S(1)}, u32[]{:S(2)}, u32[]{:S(2)}) collective-permute-start(f32[256,128]{1,0:T(8,128)S(1)} %convolution_multiply_fusion.3), channel_id=1, source_target_pairs={{0,1},{1,0},{2,3},{3,2},{4,5},{5,4},{6,7},{7,6},{8,9},{9,8},{10,11... | collective-permute-start | bytes 393224 | tf_op jit(solution)/shard_map/ppermute | solution.py:43
  62.3 1.5 %collective-permute-start.7 = (f32[8,32,128]{2,1,0:T(8,128)S(1)}, f32[8,32,128]{2,1,0:T(8,128)S(1)}, u32[]{:S(2)}, u32[]{:S(2)}) collective-permute-start(f32[8,32,128]{2,1,0:T(8,128)S(1)} %collective-permute-done.6), channel_id=1, source_target_pairs={{0,1},{1,0},{2,3},{3,2},{4,5},{5,4},{6,7},{7,6},{8,9},{9,8},{10,11... | collective-permute-start | bytes 393224 | tf_op jit(solution)/shard_map/ppermute | solution.py:43

commit v2 on v0

v2 whole, which is shorter than its diff:
```python
import functools
import math

import jax
import jax.numpy as jnp
from jax import lax
from jax.experimental import pallas as pl
from jax.experimental.pallas import tpu as pltpu
from jax.sharding import Mesh, PartitionSpec as P

STEPS = 2
STEP_SIZE = 2.0
F32, BF16 = jnp.float32, jnp.bfloat16
ROW_CHUNK = 256
SOURCE_CHUNK = 256
VMEM_LIMIT = 48 << 20


def parts(x, count):
    out = []
    for _ in range(count - 1):
        piece = x.astype(BF16)
        out.append(piece)
        x = x - piece.astype(F32)
    out.append(x.astype(BF16))
    return out


def dot(a, b):
    return jnp.dot(a, b, preferred_element_type=F32)


def dot_t(a, b):
    return lax.dot_general(a, b, (((1,), (1,)), ((), ())), preferred_element_type=F32)


def lanes(*pieces):
    return jnp.concatenate(pieces, axis=1)


def folded(x):
    half = x.shape[1] // 2
    return x[:, :half] + x[:, half:]


def grad_kernel(scale, place_ref, x_ref, rows_a_ref, rows_b_ref, targets_a_ref, targets_b_ref, out_ref):
    count = out_ref.shape[0]
    if count == x_ref.shape[0]:
        x = x_ref[...]
    else:
        x = x_ref[pl.ds(pl.multiple_of(place_ref[0] * count, count), count), :]
    high, low = parts(x, 2)
    wide = lanes(high, low, high, low)
    total = None
    for rows_ref, targets_ref in ((rows_a_ref, targets_a_ref), (rows_b_ref, targets_b_ref)):
        for start in range(0, rows_ref.shape[0], ROW_CHUNK):
            span = slice(start, start + ROW_CHUNK)
            row_high, row_low = parts(rows_ref[span, :], 2)
            logits = dot_t(wide, lanes(row_high, row_high, row_low, row_low))
            resid = targets_ref[:, span] - 1.0 / (1.0 + jnp.exp(-logits))
            resid_high, resid_low = parts(resid, 2)
            both = lanes(row_high, row_low)
            added = dot(resid_high, both) + dot(resid_low, both)
            total = added if total is None else total + added
    out_ref[...] = folded(total) * scale


def move_kernel(last, local, place_ref, spread_ref, mine_ref, pair_ref, grad_ref, pair_grad_ref, out_ref, acc_ref, kern_ref):
    dom, chip = place_ref[0], place_ref[1]
    inverse = 1.0 / spread_ref[0]
    width = mine_ref.shape[1]
    block = acc_ref.shape[0] if last else grad_ref.shape[0]
    own_span = pl.ds(pl.multiple_of(dom * block, block), block)
    aimed = mine_ref[own_span, :] if last else mine_ref[...]
    count = aimed.shape[0]
    doms = count // block
    high, mid, low = parts(aimed, 3)
    wide = lanes(high, mid, high, mid, high, low)
    square_a = jnp.sum(aimed * aimed, axis=1, keepdims=True)
    starts = [pl.multiple_of(d * block + chip * local, local) for d in range(doms)]
    if last:
        own_aimed = [mine_ref[pl.ds(pl.multiple_of(dom * block + chip * local, local), local), :]]
    else:
        own_aimed = [mine_ref[pl.ds(s, local), :] for s in starts]
    own_cubed = [jnp.zeros((local, 1), F32) for _ in starts]
    own_pulled = [jnp.zeros((local, 2 * width), F32) for _ in starts]
    ones = jnp.ones((8, 3 * width), BF16)
    first = True
    for source_ref, source_grad_ref in ((mine_ref, grad_ref), (pair_ref, pair_grad_ref)):
        for start in range(0, source_grad_ref.shape[0], SOURCE_CHUNK):
            if last:
                source = source_ref[start:start + SOURCE_CHUNK, :]
            else:
                source = source_ref[pl.ds(pl.multiple_of(dom * block + start, SOURCE_CHUNK), SOURCE_CHUNK), :]
            s_high, s_mid, s_low = parts(source, 3)
            inner = dot_t(wide, lanes(s_high, s_high, s_mid, s_mid, s_low, s_high))
            square_b = dot_t(ones, lanes(*parts(source * source, 3)))[:1, :]
            kernel = lax.rsqrt(1.0 + (square_a + square_b - 2.0 * inner) * inverse)
            kern_ref[...] = kernel
            k_high, k_low = parts(kernel, 2)
            grads = lanes(*parts(source_grad_ref[start:start + SOURCE_CHUNK, :], 2))
            drive = dot(k_high, grads) + dot(k_low, grads)
            if first:
                acc_ref[...] = drive
            else:
                acc_ref[...] += drive
            first = False
            pulls = lanes(*parts(source, 2))
            for i, s in enumerate(starts):
                own = kern_ref[pl.ds(s, local), :]
                cubed = own * own * own
                own_cubed[i] = own_cubed[i] + jnp.sum(cubed, axis=1, keepdims=True)
                w_high, w_low = parts(own + cubed * inverse, 2)
                own_pulled[i] = own_pulled[i] + dot(w_high, pulls) + dot(w_low, pulls)
    for i, s in enumerate(starts):
        extra = own_aimed[i] * (own_cubed[i] * inverse) - folded(own_pulled[i])
        acc_ref[pl.ds(s, local), :] += lanes(extra, jnp.zeros_like(extra))
    if last:
        moves = folded(acc_ref[...])
        for j in range(block // local):
            out_ref[j, :local, :] = moves[j * local:(j + 1) * local, :]
            out_ref[j, local:, :] = grad_ref[pl.ds(pl.multiple_of(dom * block + j * local, local), local), :]
    else:
        out_ref[...] = folded(acc_ref[...])


SMEM_SPEC = pl.BlockSpec(memory_space=pltpu.SMEM)
VMEM_SPEC = pl.BlockSpec(memory_space=pltpu.VMEM)
PARAMS = pltpu.CompilerParams(vmem_limit_bytes=VMEM_LIMIT)


def likelihood(place, x, count, row_sets, scale):
    (rows_a, targets_a), (rows_b, targets_b) = row_sets
    width = x.shape[1]
    data = rows_a.shape[0] + rows_b.shape[0]
    return pl.pallas_call(
        functools.partial(grad_kernel, scale),
        out_shape=jax.ShapeDtypeStruct((count, width), F32),
        in_specs=[SMEM_SPEC] + [VMEM_SPEC] * 5,
        out_specs=VMEM_SPEC,
        compiler_params=PARAMS,
        cost_estimate=pl.CostEstimate(flops=16 * count * data * width, bytes_accessed=0, transcendentals=count * data),
        name="grad",
    )(place, x, rows_a, rows_b, targets_a, targets_b)


def partial_move(place, spread, mine, pair, grads, pair_grads, block, local, last):
    width = mine.shape[1]
    count = block if last else mine.shape[0]
    shape = (block // local, 2 * local, width) if last else (count, width)
    return pl.pallas_call(
        functools.partial(move_kernel, last, local),
        out_shape=jax.ShapeDtypeStruct(shape, F32),
        in_specs=[SMEM_SPEC] * 2 + [VMEM_SPEC] * 4,
        out_specs=VMEM_SPEC,
        scratch_shapes=[pltpu.VMEM((count, 2 * width), F32), pltpu.VMEM((count, SOURCE_CHUNK), F32)],
        compiler_params=PARAMS,
        cost_estimate=pl.CostEstimate(flops=40 * count * grads.shape[0] * width, bytes_accessed=0, transcendentals=0),
        name="move",
    )(place, spread, mine, pair, grads, pair_grads)


def swapped(x):
    return lax.ppermute(x, "core", [(0, 1), (1, 0)])


def shards(positions, length_scale, features, labels, batch_index):
    doms, chips, cores = lax.axis_size("dom"), lax.axis_size("chip"), lax.axis_size("core")
    local, width = positions.shape
    block = chips * local
    scale = 1.0 / math.sqrt(batch_index.shape[0] * chips * cores)
    factor = STEP_SIZE / (local * doms * chips * cores)
    place = jnp.stack([lax.axis_index("dom"), lax.axis_index("chip")]).astype(jnp.int32)
    everywhere = ("dom", "chip")

    def spread_out(x):
        tiled = jnp.broadcast_to(x[None], (doms * chips,) + x.shape)
        return lax.all_to_all(tiled, everywhere, 0, 0, tiled=True).reshape(-1, width)

    rows = features[batch_index]
    targets = labels[batch_index].astype(F32)[None, :]
    row_sets = ((rows, targets), (swapped(rows), swapped(targets)))

    current = positions
    for iteration in range(STEPS):
        last = iteration == STEPS - 1
        mine = spread_out(current)
        pair = swapped(mine)
        grads = likelihood(place, mine, mine.shape[0] if last else block, row_sets, scale)
        pair_grads = swapped(grads)
        moves = partial_move(place, length_scale, mine, pair, grads, pair_grads, block, local, last)
        if last:
            result = jnp.sum(lax.all_to_all(moves, "chip", 0, 0, tiled=True), axis=0)
            score = result[local:] - current
            current = current + factor * result[:local]
        else:
            moves = lax.all_to_all(moves.reshape(doms * chips, local, width), everywhere, 0, 0, tiled=True)
            current = current + factor * jnp.sum(moves, axis=0)
    return (current, score)


def solution(mesh):
    doms, dp = mesh.shape["dom"], mesh.shape["dp"]
    inner = Mesh(mesh.devices.reshape(doms, dp // 2, 2), ("dom", "chip", "core"))
    dp_axes = ("chip", "core")
    placed = (P(("dom",) + dp_axes, None), P(), P(dp_axes, None), P(dp_axes), P(dp_axes))
    return jax.shard_map(
        shards,
        mesh=inner,
        in_specs=placed,
        out_specs=(P(("dom",) + dp_axes, None), P(("dom",) + dp_axes, None)),
        check_vma=False,
    )
```

time: 273 us -> 73 us (0.27)
  waiting for transfers between devices: 183 us -> 6.71 us
  blocking collectives: 55 us -> 38.5 us
  between operations: 14.5 us -> 1.43 us
  matrix products: 10.8 us -> 0 us
  starting transfers between devices: 0.16 us -> 10.2 us
  Pallas kernels: 0 us -> 8.41 us
  other arithmetic: 3.51 us -> 0.75 us
    psum x2 -> x0, waiting for transfers between devices: 163 us -> none  [shards(): gradient_block = lax.psum(likelihood(block, rows, targets, scale), 'dp')]
    all_gather x4 -> x0, blocking collectives: 55 us -> none  [the longest x2 46.2 us: shards(): block = lax.all_gather(current, 'dp', axis=0, tiled=True)]
    all_to_all x0 -> x3, blocking collectives: none -> 38.5 us  [the longest x1 13.6 us: shards(): lax.all_to_all(moves.reshape(doms * chips, local, width), everywhere, 0,...]
    reduce_scatter x2 -> x0, waiting for transfers between devices: 20.6 us -> none  [shards(): lax.psum_scatter(displace(aimed_all, block, score_block, spread), 'dom',...]
    dot_general x10 -> x0, matrix products: 10.8 us -> none  [the longest x2 4.23 us: likelihood(): jnp.dot(resid, rows, precision=HIGH, preferred_element_type=jnp.float32)]
    all_to_all x0 -> x1, starting transfers between devices: none -> 8.47 us  [spread_out(): lax.all_to_all(tiled, everywhere, 0, 0, tiled=True).reshape(-1, width)]
    pallas_call x0 -> x4, Pallas kernels: none -> 8.41 us  [the longest x2 4.65 us: partial_move(): pl.pallas_call(functools.partial(move_kernel, last, local), out_shape=jax...]
    all_to_all x0 -> x1, waiting for transfers between devices: none -> 4.97 us  [spread_out(): lax.all_to_all(tiled, everywhere, 0, 0, tiled=True).reshape(-1, width)]
  transfers between devices with their start and end apart: 4 -> 7, of which waited for: 4 -> 4; matrix products, arithmetic and copies ran while one was open for 1% -> 6% of each run, Pallas kernels for 0% -> 2%
where the time goes in v2:
time: 73 us; the launch traced here: 72.5 us
  blocking collectives  38.5 us (53%)
  starting transfers between devices  10.2 us (14%)
  Pallas kernels  8.41 us (12%)
  waiting for transfers between devices  6.71 us (9%)
  local copies, waits for them, and re-layouts  6.44 us (9%)
  between operations  1.43 us (2%)
  other arithmetic  0.75 us (1%)
    all_to_all x1, blocking collectives, shards(): lax.all_to_all(moves.reshape(doms * chips, local, width), everywhere, 0,...  13.6 us
    all_to_all x1, blocking collectives, spread_out(): lax.all_to_all(tiled, everywhere, 0, 0, tiled=True).reshape(-1, width)  12.7 us
    all_to_all x1, blocking collectives, shards(): result = jnp.sum(lax.all_to_all(moves, 'chip', 0, 0, tiled=True), axis=0)  12.3 us
    all_to_all x1, starting transfers between devices, spread_out(): lax.all_to_all(tiled, everywhere, 0, 0, tiled=True).reshape(-1, width)  8.47 us
    all_to_all x1, waiting for transfers between devices, spread_out(): lax.all_to_all(tiled, everywhere, 0, 0, tiled=True).reshape(-1, width)  4.97 us
    pallas_call x2, Pallas kernels, partial_move(): pl.pallas_call(functools.partial(move_kernel, last, local), out_shape=jax...  4.65 us
    pallas_call x2, Pallas kernels, likelihood(): pl.pallas_call(functools.partial(grad_kernel, scale), out_shape=jax.Shape...  3.76 us
    gather x1, local copies, waits for them, and re-layouts, shards(): targets = labels[batch_index].astype(F32)[None, :]  3.14 us
  transfers between devices with their start and end apart: 7, of which 4 were waited for; matrix products, arithmetic and copies ran while one was open for 6% of the time, Pallas kernels for 2%

profile of v2, /device:TPU:0, one launch (start us, length us, event | category | flops | bytes accessed | tf_op | source)
XLA Modules:
  0.0 72.5 jit_solution(5050958608409267777)
XLA Ops:
  0.6 0.0 copy-start
  0.6 1.5 %broadcast_in_dim.6 = f32[16,32,128]{2,1,0:T(8,128)} broadcast(f32[32,128]{1,0:T(8,128)} %param.5), dimensions={1,2} | broadcast | bytes 278528 | tf_op jit(solution)/shard_map/broadcast_in_dim | solution.py:177
  2.2 0.0 copy-start.3
  2.2 8.5 %all-to-all-start = ((f32[16,32,128]{2,1,0:T(8,128)}), f32[16,32,128]{2,1,0:T(8,128)S(1)}, u32[]{:S(2)}, u32[]{:S(2)}) async-start(f32[16,32,128]{2,1,0:T(8,128)} %broadcast_in_dim.6), calls=%async_computation | async-start | bytes 524288 | tf_op jit(solution)/shard_map/all_to_all | solution.py:178
  10.7 0.0 copy-done.3
  10.7 0.0 copy-done
  10.7 0.0 copy-start.1
  10.7 1.0 %gather_fusion = f32[512,128]{1,0:T(8,128)S(1)} fusion(f32[2048,128]{1,0:T(8,128)S(1)} %copy-done, s32[1024]{0:T(1024)S(1)} %pad_clamp_fusion), kind=kCustom, calls=%fused_computation | custom fusion | bytes 526336 | tf_op jit(solution)/shard_map/gather | solution.py:180
  11.8 0.1 collective-permute-start.1
  11.8 0.0 copy-done.1
  11.8 3.1 %gather_fusion.1 = s32[512]{0:T(512)S(1)} fusion(s32[2048]{0:T(1024)S(1)} %copy-done.1, s32[1024]{0:T(1024)S(1)} %pad_clamp_fusion), kind=kCustom, calls=%fused_computation.1 | custom fusion | bytes 6144 | tf_op jit(solution)/shard_map/gather | solution.py:181
  15.0 0.5 collective-permute-start.2
  15.6 5.0 %all-to-all-done = f32[16,32,128]{2,1,0:T(8,128)S(1)} async-done(((f32[16,32,128]{2,1,0:T(8,128)}), f32[16,32,128]{2,1,0:T(8,128)S(1)}, u32[]{:S(2)}, u32[]{:S(2)}) %all-to-all-start) | async-done | bytes 262176 | tf_op jit(solution)/shard_map/all_to_all | solution.py:178
  20.5 0.0 collective-permute-start
  20.5 0.1 pad_add_fusion.place_ref
  20.6 0.0 collective-permute-done.2.targets_b_ref
  20.6 0.0 collective-permute-done.1.rows_b_ref
  20.6 1.6 %grad.2.grad_ref = f32[256,128]{1,0:T(8,128)S(1)} custom-call(s32[2]{0:T(128)S(1)} %pad_add_fusion.place_ref, f32[512,128]{1,0:T(8,128)S(1)} %bitcast.7, f32[512,128]{1,0:T(8,128)S(1)} %gather_fusion, f32[512,128]{1,0:T(8,128)S(1)} %collective-permute-done.1.rows_b_ref, f32[1,512]{1,0:T(1,128)S(1)} %bitcast.14, f32[1,512]{1,0:T(1,128)S(1)} %collective-permute-done.2.targets_b_ref), custom_call_target="tpu_custom_call" | custom-call | flops 536870912 | tf_op jit(solution)/shard_map/grad/pallas_call | solution.py:136
  22.2 0.6 collective-permute-start.3
  23.4 0.3 collective-permute-done.3.pair_grad_ref
  23.8 0.0 collective-permute-done.pair_ref
  23.8 2.1 %move.2 = f32[512,128]{1,0:T(8,128)S(1)} custom-call(s32[2]{0:T(128)S(1)} %pad_add_fusion.place_ref, f32[1]{0:T(128)S(6)} %copy.7.spread_ref, f32[512,128]{1,0:T(8,128)S(1)} %bitcast.8, f32[512,128]{1,0:T(8,128)S(1)} %collective-permute-done.pair_ref, f32[256,128]{1,0:T(8,128)S(1)} %grad.2.grad_ref, f32[256,128]{1,0:T(8,128)S(1)} %collective-permute-done.3.pair_grad_ref), custom_call_target="tpu_custom_call" | custom-call | flops 671088640 | tf_op jit(solution)/shard_map/move/pallas_call | solution.py:151
  25.9 13.6 %all_to_all.20 = f32[16,32,128]{2,1,0:T(8,128)S(1)} all-to-all(f32[16,32,128]{2,1,0:T(8,128)S(1)} %bitcast.12), channel_id=1, replica_groups=mesh['dom'=2,'chip'=8,'core'=2] {'dom','chip'}, dimensions={0} | all-to-all | bytes 524288 | tf_op jit(solution)/shard_map/all_to_all | solution.py:197
  39.5 0.0 copy-start.2
  39.5 0.7 copy-done.2
  40.2 12.7 %all_to_all.21 = f32[16,32,128]{2,1,0:T(8,128)S(1)} all-to-all(f32[16,32,128]{2,1,0:T(8,128)S(1)} %broadcast_in_dim.8), channel_id=1, replica_groups=mesh['dom'=2,'chip'=8,'core'=2] {'dom','chip'}, dimensions={0} | all-to-all | bytes 524288 | tf_op jit(solution)/shard_map/all_to_all | solution.py:178
  52.9 2.2 %grad.3.grad_ref = f32[512,128]{1,0:T(8,128)S(1)} custom-call(s32[2]{0:T(128)S(1)} %pad_add_fusion.place_ref, f32[512,128]{1,0:T(8,128)S(1)} %bitcast.9, f32[512,128]{1,0:T(8,128)S(1)} %gather_fusion, f32[512,128]{1,0:T(8,128)S(1)} %collective-permute-done.1.rows_b_ref, f32[1,512]{1,0:T(1,128)S(1)} %bitcast.15, f32[1,512]{1,0:T(1,128)S(1)} %collective-permute-done.2.targets_b_ref), custom_call_target="tpu_custom_call" | custom-call | flops 1073741824 | tf_op jit(solution)/shard_map/grad/pallas_call | solution.py:136
  55.1 0.1 collective-permute-start.5
  55.1 0.5 collective-permute-start.4
  55.6 1.0 %collective-permute-done.5.pair_grad_ref = f32[512,128]{1,0:T(8,128)S(1)} collective-permute-done((f32[512,128]{1,0:T(8,128)S(1)}, f32[512,128]{1,0:T(8,128)S(1)}, u32[]{:S(2)}, u32[]{:S(2)}) %collective-permute-start.5) | collective-permute-done | bytes 262176 | tf_op jit(solution)/shard_map/ppermute | solution.py:164
  56.7 0.4 collective-permute-done.4.pair_ref
  57.0 2.5 %move.3 = f32[8,64,128]{2,1,0:T(8,128)S(1)} custom-call(s32[2]{0:T(128)S(1)} %pad_add_fusion.place_ref, f32[1]{0:T(128)S(6)} %copy.7.spread_ref, f32[512,128]{1,0:T(8,128)S(1)} %bitcast.11, f32[512,128]{1,0:T(8,128)S(1)} %collective-permute-done.4.pair_ref, f32[512,128]{1,0:T(8,128)S(1)} %grad.3.grad_ref, f32[512,128]{1,0:T(8,128)S(1)} %collective-permute-done.5.pair_grad_ref), custom_call_target="tpu_custom_call" | custom-call | flops 671088640 | tf_op jit(solution)/shard_map/move/pallas_call | solution.py:151
  59.6 12.3 %all_to_all.22 = f32[8,64,128]{2,1,0:T(8,128)S(1)} all-to-all(f32[8,64,128]{2,1,0:T(8,128)S(1)} %move.3), channel_id=1, replica_groups=mesh['dom'=2,'chip'=8,'core'=2] {'chip'}, dimensions={0} | all-to-all | bytes 524288 | tf_op jit(solution)/shard_map/all_to_all | solution.py:193
  71.9 0.6 slice_subtract_fusion
  (7 shorter events, 0.1 us)
Async XLA Ops:
  0.6 10.1 %copy-start = (f32[2048,128]{1,0:T(8,128)S(1)}, f32[2048,128]{1,0:T(8,128)}, u32[]{:S(2)}) copy-start(f32[2048,128]{1,0:T(8,128)} %param.7) | copy-start | bytes 3145732
  2.2 8.5 %copy-start.3 = (s32[512]{0:T(512)S(1)}, s32[512]{0:T(512)}, u32[]{:S(2)}) copy-start(s32[512]{0:T(512)} %param.9) | copy-start | bytes 6148
  2.2 18.4 %all-to-all-start = ((f32[16,32,128]{2,1,0:T(8,128)}), f32[16,32,128]{2,1,0:T(8,128)S(1)}, u32[]{:S(2)}, u32[]{:S(2)}) async-start(f32[16,32,128]{2,1,0:T(8,128)} %broadcast_in_dim.6), calls=%async_computation | async-start | bytes 524288 | tf_op jit(solution)/shard_map/all_to_all | solution.py:178
  10.7 1.1 %copy-start.1 = (s32[2048]{0:T(1024)S(1)}, s32[2048]{0:T(1024)}, u32[]{:S(2)}) copy-start(s32[2048]{0:T(1024)} %param.8) | copy-start | bytes 24580
  11.8 8.9 %collective-permute-start.1 = (f32[512,128]{1,0:T(8,128)S(1)}, f32[512,128]{1,0:T(8,128)S(1)}, u32[]{:S(2)}, u32[]{:S(2)}) collective-permute-start(f32[512,128]{1,0:T(8,128)S(1)} %gather_fusion), channel_id=1, source_target_pairs={{0,1},{1,0},{2,3},{3,2},{4,5},{5,4},{6,7},{7,6},{8,9},{9,8},{10,11... | collective-permute-start | bytes 786440 | tf_op jit(solution)/shard_map/ppermute | solution.py:164
  15.0 5.6 %collective-permute-start.2 = (f32[1,512]{1,0:T(1,128)S(1)}, f32[1,512]{1,0:T(1,128)S(1)}, u32[]{:S(2)}, u32[]{:S(2)}) collective-permute-start(f32[1,512]{1,0:T(1,128)S(1)} %bitcast.13), channel_id=1, source_target_pairs={{0,1},{1,0},{2,3},{3,2},{4,5},{5,4},{6,7},{7,6},{8,9},{9,8},{10,11... | collective-permute-start | bytes 6152 | tf_op jit(solution)/shard_map/ppermute | solution.py:164
  20.5 3.3 %collective-permute-start = (f32[512,128]{1,0:T(8,128)S(1)}, f32[512,128]{1,0:T(8,128)S(1)}, u32[]{:S(2)}, u32[]{:S(2)}) collective-permute-start(f32[512,128]{1,0:T(8,128)S(1)} %bitcast.6), channel_id=1, source_target_pairs={{0,1},{1,0},{2,3},{3,2},{4,5},{5,4},{6,7},{7,6},{8,9},{9,8},{10,11... | collective-permute-start | bytes 786440 | tf_op jit(solution)/shard_map/ppermute | solution.py:164
  22.2 1.6 %collective-permute-start.3 = (f32[256,128]{1,0:T(8,128)S(1)}, f32[256,128]{1,0:T(8,128)S(1)}, u32[]{:S(2)}, u32[]{:S(2)}) collective-permute-start(f32[256,128]{1,0:T(8,128)S(1)} %grad.2.grad_ref), channel_id=1, source_target_pairs={{0,1},{1,0},{2,3},{3,2},{4,5},{5,4},{6,7},{7,6},{8,9},{9,8},{10,11... | collective-permute-start | bytes 393224 | tf_op jit(solution)/shard_map/ppermute | solution.py:164
  39.5 0.7 copy-start.2
  55.1 1.6 %collective-permute-start.5 = (f32[512,128]{1,0:T(8,128)S(1)}, f32[512,128]{1,0:T(8,128)S(1)}, u32[]{:S(2)}, u32[]{:S(2)}) collective-permute-start(f32[512,128]{1,0:T(8,128)S(1)} %grad.3.grad_ref), channel_id=1, source_target_pairs={{0,1},{1,0},{2,3},{3,2},{4,5},{5,4},{6,7},{7,6},{8,9},{9,8},{10,11... | collective-permute-start | bytes 786440 | tf_op jit(solution)/shard_map/ppermute | solution.py:164
  55.1 1.9 %collective-permute-start.4 = (f32[512,128]{1,0:T(8,128)S(1)}, f32[512,128]{1,0:T(8,128)S(1)}, u32[]{:S(2)}, u32[]{:S(2)}) collective-permute-start(f32[512,128]{1,0:T(8,128)S(1)} %bitcast.10), channel_id=1, source_target_pairs={{0,1},{1,0},{2,3},{3,2},{4,5},{5,4},{6,7},{7,6},{8,9},{9,8},{10,11... | collective-permute-start | bytes 786440 | tf_op jit(solution)/shard_map/ppermute | solution.py:164

commit v3 on v0

v3 whole, which is shorter than its diff:
```python
import functools
import math

import jax
import jax.numpy as jnp
from jax import lax
from jax.experimental import pallas as pl
from jax.experimental.pallas import tpu as pltpu
from jax.sharding import Mesh, PartitionSpec as P

STEPS = 2
STEP_SIZE = 2.0
F32, BF16 = jnp.float32, jnp.bfloat16
ROW_CHUNK = 256
SOURCE_CHUNK = 256
VMEM_LIMIT = 32 << 20
LANES = 128


def parts(x, count):
    out = []
    for _ in range(count - 1):
        piece = x.astype(BF16)
        out.append(piece)
        x = x - piece.astype(F32)
    out.append(x.astype(BF16))
    return out


def dot(a, b):
    return jnp.dot(a, b, preferred_element_type=F32)


def dot_t(a, b):
    return lax.dot_general(a, b, (((1,), (1,)), ((), ())), preferred_element_type=F32)


def lanes(*pieces):
    return jnp.concatenate(pieces, axis=1)


def folded(x):
    half = x.shape[1] // 2
    return x[:, :half] + x[:, half:]


def chunks(refs, size):
    for ref in refs:
        for start in range(0, ref.shape[0], size):
            yield ref[start:start + size, :]


def tile_kernel(x_ref, out_ref):
    out_ref[...] = jnp.broadcast_to(x_ref[...][None], out_ref.shape)


def grad_kernel(scale, x_ref, rows_a_ref, rows_b_ref, targets_ref, out_ref):
    high, low = parts(-x_ref[...], 2)
    wide = lanes(high, low, high, low)
    total, start = None, 0
    for rows in chunks((rows_a_ref, rows_b_ref), ROW_CHUNK):
        row_high, row_low = parts(rows, 2)
        minus_logits = dot_t(wide, lanes(row_high, row_high, row_low, row_low))
        targets = targets_ref[:, start:start + rows.shape[0]]
        start += rows.shape[0]
        resid_high, resid_low = parts(targets - 1.0 / (1.0 + jnp.exp(minus_logits)), 2)
        both = lanes(row_high, row_low)
        added = dot(resid_high, both) + dot(resid_low, both)
        total = added if total is None else total + added
    out_ref[...] = folded(total) * scale


def kernel_of(aimed, inverse):
    high, mid, low = parts(aimed * (-2.0 * inverse), 3)
    wide = lanes(high, mid, high, mid, high, low)
    square_a = 1.0 + jnp.sum(aimed * aimed, axis=1, keepdims=True) * inverse
    ones = jnp.ones((8, 3 * aimed.shape[1]), BF16)

    def with_sources(source):
        s_high, s_mid, s_low = parts(source, 3)
        inner = dot_t(wide, lanes(s_high, s_high, s_mid, s_mid, s_low, s_high))
        square_b = dot_t(ones, lanes(*parts(source * source, 3)))[:1, :] * inverse
        return lax.rsqrt((square_a + square_b) + inner), lanes(s_high, s_mid)

    return with_sources


def weights_kernel(spread_ref, aimed_ref, *refs):
    source_refs, (high_ref, low_ref) = refs[:-2], refs[-2:]
    with_sources = kernel_of(aimed_ref[...], 1.0 / spread_ref[...])
    start = 0
    for source in chunks(source_refs, SOURCE_CHUNK):
        span = slice(start, start + source.shape[0])
        high_ref[:, span], low_ref[:, span] = parts(with_sources(source)[0], 2)
        start += source.shape[0]


def drive_kernel(local, high_ref, low_ref, *refs):
    grad_refs, riders, out_ref = refs[:2], refs[2:-1], refs[-1]
    grads = jnp.concatenate([lanes(*parts(ref[...], 2)) for ref in grad_refs], axis=0)
    drive = folded(dot(high_ref[...], grads) + dot(low_ref[...], grads))
    if not riders:
        out_ref[...] = drive
        return
    for j in range(out_ref.shape[0]):
        out_ref[j, :local, :] = drive[j * local:(j + 1) * local, :]
        out_ref[j, local:, :] = riders[0][j * local:(j + 1) * local, :]


def own_kernel(spread_ref, own_ref, *refs):
    source_refs, out_ref = refs[:-1], refs[-1]
    inverse = 1.0 / spread_ref[...]
    own = own_ref[...]
    with_sources = kernel_of(own, inverse)
    cubes, pulled = None, None
    for source in chunks(source_refs, SOURCE_CHUNK):
        kernel, pulls = with_sources(source)
        cubed = kernel * kernel * kernel
        high, low = parts(kernel + cubed * inverse, 2)
        cube, pull = jnp.sum(cubed, axis=1, keepdims=True), dot(high, pulls) + dot(low, pulls)
        cubes, pulled = (cube, pull) if cubes is None else (cubes + cube, pulled + pull)
    out_ref[...] = own * (cubes * inverse) - folded(pulled)


VMEM_SPEC = pl.BlockSpec(memory_space=pltpu.VMEM)


def run(kernel, out_shape, *args, flops=0):
    moved = sum(math.prod(a.shape) for a in args) * 4
    return pl.pallas_call(
        kernel,
        out_shape=out_shape,
        in_specs=[VMEM_SPEC] * len(args),
        out_specs=jax.tree.map(lambda _: VMEM_SPEC, out_shape),
        compiler_params=pltpu.CompilerParams(vmem_limit_bytes=VMEM_LIMIT),
        cost_estimate=pl.CostEstimate(flops=flops, bytes_accessed=moved, transcendentals=0),
    )(*args)


def array(*shape, dtype=F32):
    return jax.ShapeDtypeStruct(shape, dtype)


def swapped(x):
    return lax.ppermute(x, "core", [(0, 1), (1, 0)])


def picked(table, index):
    grid = table.astype(BF16).reshape(-1, LANES)
    major = lax.broadcasted_iota(jnp.int32, (grid.shape[0], index.shape[0]), 0) == (index // LANES)[None, :]
    minor = lax.broadcasted_iota(jnp.int32, (LANES, index.shape[0]), 0) == (index % LANES)[None, :]
    found = lax.dot_general(grid, major.astype(BF16), (((0,), (0,)), ((), ())), preferred_element_type=F32)
    return jnp.sum(jnp.where(minor, found, 0.0), axis=0, keepdims=True)


def shards(positions, length_scale, features, labels, batch_index):
    doms, chips, cores = lax.axis_size("dom"), lax.axis_size("chip"), lax.axis_size("core")
    local, width = positions.shape
    block = chips * local
    scale = 1.0 / math.sqrt(batch_index.shape[0] * chips * cores)
    factor = STEP_SIZE / (local * doms * chips * cores)
    dom, chip = lax.axis_index("dom"), lax.axis_index("chip")
    everywhere = ("dom", "chip")
    spread = length_scale.reshape(1, 1)

    rows = features[batch_index]
    targets = picked(labels, batch_index)
    pair_targets = swapped(targets)
    targets = jnp.concatenate([targets, pair_targets], axis=1)
    row_sets = (rows, swapped(rows), targets)
    data = rows.shape[0] * cores

    current = positions
    for iteration in range(STEPS):
        last = iteration == STEPS - 1
        if iteration == 0:
            tiled = run(tile_kernel, array(doms * chips, local, width), current)
        else:
            tiled = jnp.broadcast_to(current[None], (doms * chips, local, width))
        mine = lax.all_to_all(tiled, everywhere, 0, 0, tiled=True).reshape(-1, width)
        own_block = lax.dynamic_slice_in_dim(mine, dom * block, block, 0)
        if iteration == 0:
            current = lax.dynamic_slice_in_dim(own_block, chip * local, local, 0)
        pair = swapped(mine)
        if last:
            aimed, graded, sources = own_block, mine, (mine, pair)
        else:
            pair_block = lax.dynamic_slice_in_dim(pair, dom * block, block, 0)
            aimed, graded, sources = mine, own_block, (own_block, pair_block)
        count, found = aimed.shape[0], sum(s.shape[0] for s in sources)
        grads = run(
            functools.partial(grad_kernel, scale), array(graded.shape[0], width), graded, *row_sets,
            flops=16 * graded.shape[0] * data * width,
        )
        pair_grads = swapped(grads)
        high, low = run(
            weights_kernel, (array(count, found, dtype=BF16),) * 2, spread, aimed, *sources,
            flops=12 * count * found * width,
        )
        drive = functools.partial(drive_kernel, local)
        flops = 8 * count * found * width
        if last:
            rider = lax.dynamic_slice_in_dim(grads, dom * block, block, 0)
            shape = array(chips, 2 * local, width)
            moves = run(drive, shape, high, low, grads, pair_grads, rider, flops=flops)
        else:
            moves = run(drive, array(count, width), high, low, grads, pair_grads, flops=flops)
        moves = lax.all_to_all(
            moves.reshape(-1, moves.shape[-2] if last else local, width),
            "chip" if last else everywhere, 0, 0, tiled=True,
        )
        extra = run(own_kernel, array(local, width), spread, current, mine, pair, flops=flops // chips)
        result = jnp.sum(moves, axis=0)
        if last:
            score = result[local:] - current
        current = current + factor * (result[:local] + extra)
    return (current, score)


def solution(mesh):
    doms, dp = mesh.shape["dom"], mesh.shape["dp"]
    inner = Mesh(mesh.devices.reshape(doms, dp // 2, 2), ("dom", "chip", "core"))
    dp_axes = ("chip", "core")
    placed = (P(("dom",) + dp_axes, None), P(), P(dp_axes, None), P(dp_axes), P(dp_axes))
    return jax.shard_map(
        shards,
        mesh=inner,
        in_specs=placed,
        out_specs=(P(("dom",) + dp_axes, None), P(("dom",) + dp_axes, None)),
        check_vma=False,
    )
```

time: 273 us -> 70 us (0.26)
  waiting for transfers between devices: 183 us -> 25 us
  blocking collectives: 55 us -> 12.6 us
  starting transfers between devices: 0.16 us -> 17.2 us
  between operations: 14.5 us -> 1.51 us
  matrix products: 10.8 us -> 0.24 us
  Pallas kernels: 0 us -> 10.3 us
  local copies, waits for them, and re-layouts: 5.33 us -> 1.93 us
  other arithmetic: 3.51 us -> 0.7 us
    psum x2 -> x0, waiting for transfers between devices: 163 us -> none  [shards(): gradient_block = lax.psum(likelihood(block, rows, targets, scale), 'dp')]
    all_gather x4 -> x0, blocking collectives: 55 us -> none  [the longest x2 46.2 us: shards(): block = lax.all_gather(current, 'dp', axis=0, tiled=True)]
    all_to_all x0 -> x3, waiting for transfers between devices: none -> 24.5 us  [the longest x2 17.3 us: shards(): lax.all_to_all(moves.reshape(-1, moves.shape[-2] if last else local, widt...]
    reduce_scatter x2 -> x0, waiting for transfers between devices: 20.6 us -> none  [shards(): lax.psum_scatter(displace(aimed_all, block, score_block, spread), 'dom',...]
    all_to_all x0 -> x3, starting transfers between devices: none -> 15.4 us  [the longest x1 8.47 us: shards(): lax.all_to_all(tiled, everywhere, 0, 0, tiled=True).reshape(-1, width)]
    all_to_all x0 -> x1, blocking collectives: none -> 12.6 us  [shards(): lax.all_to_all(tiled, everywhere, 0, 0, tiled=True).reshape(-1, width)]
    dot_general x10 -> x1, matrix products: 10.8 us -> 0.24 us  [picked(): lax.dot_general(grid, major.astype(BF16), (((0,), (0,)), ((), ())), prefe...]
    pallas_call x0 -> x9, Pallas kernels: none -> 10.3 us  [run(): pl.pallas_call(kernel, out_shape=out_shape, in_specs=[VMEM_SPEC] * len(ar...]
  transfers between devices with their start and end apart: 4 -> 9, of which waited for: 4 -> 5; matrix products, arithmetic and copies ran while one was open for 1% -> 2% of each run, Pallas kernels for 0% -> 10%
where the time goes in v3:
time: 70 us; the launch traced here: 69.5 us
  waiting for transfers between devices  25 us (36%)
  starting transfers between devices  17.2 us (25%)
  blocking collectives  12.6 us (18%)
  Pallas kernels  10.3 us (15%)
  local copies, waits for them, and re-layouts  1.93 us (3%)
  between operations  1.51 us (2%)
    all_to_all x2, waiting for transfers between devices, shards(): lax.all_to_all(moves.reshape(-1, moves.shape[-2] if last else local, widt...  17.3 us
    all_to_all x1, blocking collectives, shards(): lax.all_to_all(tiled, everywhere, 0, 0, tiled=True).reshape(-1, width)  12.6 us
    pallas_call x9, Pallas kernels, run(): pl.pallas_call(kernel, out_shape=out_shape, in_specs=[VMEM_SPEC] * len(ar...  10.3 us
    all_to_all x1, starting transfers between devices, shards(): lax.all_to_all(tiled, everywhere, 0, 0, tiled=True).reshape(-1, width)  8.47 us
    all_to_all x1, waiting for transfers between devices, shards(): lax.all_to_all(tiled, everywhere, 0, 0, tiled=True).reshape(-1, width)  7.23 us
    all_to_all x2, starting transfers between devices, shards(): lax.all_to_all(moves.reshape(-1, moves.shape[-2] if last else local, widt...  6.94 us
    ppermute x6, starting transfers between devices, swapped(): return lax.ppermute(x, 'core', [(0, 1), (1, 0)])  1.78 us
  transfers between devices with their start and end apart: 9, of which 5 were waited for; matrix products, arithmetic and copies ran while one was open for 2% of the time, Pallas kernels for 10%

profile of v3, /device:TPU:0, one launch (start us, length us, event | category | flops | bytes accessed | tf_op | source)
XLA Modules:
  0.0 69.5 jit_solution(15733835130994900538)
XLA Ops:
  0.6 0.0 copy-start
  0.6 0.0 copy-start.1
  0.7 0.8 %copy-done.1 = f32[32,128]{1,0:T(8,128)S(1)} copy-done((f32[32,128]{1,0:T(8,128)S(1)}, f32[32,128]{1,0:T(8,128)}, u32[]{:S(2)}) %copy-start.1) | copy-done | bytes 16408
  1.5 0.7 %shard_map.68 = f32[16,32,128]{2,1,0:T(8,128)} custom-call(f32[32,128]{1,0:T(8,128)S(1)} %copy-done.1), custom_call_target="tpu_custom_call" | custom-call | bytes 16384 | tf_op jit(solution)/shard_map/pallas_call | solution.py:130
  2.2 0.0 copy-start.2
  2.2 8.5 %all-to-all-start = ((f32[16,32,128]{2,1,0:T(8,128)}), f32[16,32,128]{2,1,0:T(8,128)S(1)}, u32[]{:S(2)}, u32[]{:S(2)}) async-start(f32[16,32,128]{2,1,0:T(8,128)} %shard_map.68), calls=%async_computation | async-start | bytes 524288 | tf_op jit(solution)/shard_map/all_to_all | solution.py:180
  10.7 0.0 copy-done.2
  10.7 0.0 copy-done
  10.7 0.0 copy-start.3
  10.7 1.0 %gather_fusion = f32[512,128]{1,0:T(8,128)S(1)} fusion(f32[2048,128]{1,0:T(8,128)S(1)} %copy-done, s32[1024]{0:T(1024)S(1)} %pad_clamp_fusion), kind=kCustom, calls=%fused_computation | custom fusion | bytes 526336 | tf_op jit(solution)/shard_map/gather | solution.py:166
  11.8 0.1 collective-permute-start.1
  11.9 0.0 copy-done.3
  11.9 0.2 fusion.1
  12.1 0.6 collective-permute-start.2
  13.3 7.2 %all-to-all-done = f32[16,32,128]{2,1,0:T(8,128)S(1)} async-done(((f32[16,32,128]{2,1,0:T(8,128)}), f32[16,32,128]{2,1,0:T(8,128)S(1)}, u32[]{:S(2)}, u32[]{:S(2)}) %all-to-all-start) | async-done | bytes 262176 | tf_op jit(solution)/shard_map/all_to_all | solution.py:180
  20.5 0.0 collective-permute-start
  20.5 0.0 collective-permute-done.2
  20.6 0.0 collective-permute-done.1.rows_b_ref
  20.6 1.1 %shard_map.70.refs_0_ = f32[256,128]{1,0:T(8,128)S(1)} custom-call(f32[256,128]{1,0:T(8,128)S(1)} %constant_dynamic-slice_fusion.3.refs_0_.x_ref, f32[512,128]{1,0:T(8,128)S(1)} %gather_fusion, f32[512,128]{1,0:T(8,128)S(1)} %collective-permute-done.1.rows_b_ref, f32[1,1024]{1,0:T(1,128)S(1)} %pad_maximum_fusion.targets_ref), custom_call_target="tpu_custom_call" | custom-call | flops 536870912 | bytes 659456 | tf_op jit(solution)/shard_map/pallas_call | solution.py:130
  21.6 0.6 collective-permute-start.3
  22.2 0.0 collective-permute-done.refs_1_
  22.2 0.8 %shard_map.69 = (bf16[512,512]{1,0:T(8,128)(2,1)S(1)}, bf16[512,512]{1,0:T(8,128)(2,1)S(1)}) custom-call(f32[1,1]{1,0:T(1,128)} %bitcast.14.spread_ref, f32[512,128]{1,0:T(8,128)S(1)} %bitcast.20, f32[256,128]{1,0:T(8,128)S(1)} %constant_dynamic-slice_fusion.3.refs_0_.x_ref, f32[256,128]{1,0:T(8,128)S(1)} %constant_dynamic-slice_fusion.2.refs_1_), custom_call_target="tpu_custom_call" | custom-call | flops 402653184 | bytes 524292 | tf_op jit(solution)/shard_map/pallas_call | solution.py:130
  23.0 0.2 collective-permute-done.3.refs_1_
  23.2 1.1 %shard_map.71 = f32[512,128]{1,0:T(8,128)} custom-call(bf16[512,512]{1,0:T(8,128)(2,1)S(1)} %get-tuple-element.6.high_ref, bf16[512,512]{1,0:T(8,128)(2,1)S(1)} %get-tuple-element.7.low_ref, f32[256,128]{1,0:T(8,128)S(1)} %shard_map.70.refs_0_, f32[256,128]{1,0:T(8,128)S(1)} %collective-permute-done.3.refs_1_), custom_call_target="tpu_custom_call" | custom-call | flops 268435456 | bytes 2359296 | tf_op jit(solution)/shard_map/pallas_call | solution.py:130
  24.4 3.5 %all-to-all-start.1 = ((f32[16,32,128]{2,1,0:T(8,128)}), f32[16,32,128]{2,1,0:T(8,128)S(1)}, u32[]{:S(2)}, u32[]{:S(2)}) async-start(f32[16,32,128]{2,1,0:T(8,128)} %bitcast.5), calls=%async_computation.1 | async-start | bytes 524288 | tf_op jit(solution)/shard_map/all_to_all | solution.py:208
  27.9 1.5 %shard_map.72 = f32[32,128]{1,0:T(8,128)S(1)} custom-call(f32[1,1]{1,0:T(1,128)} %bitcast.15.spread_ref, f32[32,128]{1,0:T(8,128)S(1)} %constant_dynamic-slice_fusion.4.own_ref, f32[512,128]{1,0:T(8,128)S(1)} %bitcast.22, f32[512,128]{1,0:T(8,128)S(1)} %collective-permute-done.refs_1_), custom_call_target="tpu_custom_call" | custom-call | flops 33554432 | bytes 540676 | tf_op jit(solution)/shard_map/pallas_call | solution.py:130
  29.4 9.1 %all-to-all-done.1 = f32[16,32,128]{2,1,0:T(8,128)S(1)} async-done(((f32[16,32,128]{2,1,0:T(8,128)}), f32[16,32,128]{2,1,0:T(8,128)S(1)}, u32[]{:S(2)}, u32[]{:S(2)}) %all-to-all-start.1) | async-done | bytes 262176 | tf_op jit(solution)/shard_map/all_to_all | solution.py:208
  38.6 12.6 %all_to_all.20 = f32[16,32,128]{2,1,0:T(8,128)S(1)} all-to-all(f32[16,32,128]{2,1,0:T(8,128)S(1)} %broadcast_in_dim.21), channel_id=1, replica_groups=mesh['dom'=2,'chip'=8,'core'=2] {'dom','chip'}, dimensions={0} | all-to-all | bytes 524288 | tf_op jit(solution)/shard_map/all_to_all | solution.py:180
  51.2 0.0 collective-permute-start.4
  51.2 1.6 %shard_map.74.refs_0_ = f32[512,128]{1,0:T(8,128)S(1)} custom-call(f32[512,128]{1,0:T(8,128)S(1)} %bitcast.25, f32[512,128]{1,0:T(8,128)S(1)} %gather_fusion, f32[512,128]{1,0:T(8,128)S(1)} %collective-permute-done.1.rows_b_ref, f32[1,1024]{1,0:T(1,128)S(1)} %pad_maximum_fusion.targets_ref), custom_call_target="tpu_custom_call" | custom-call | flops 1073741824 | bytes 790528 | tf_op jit(solution)/shard_map/pallas_call | solution.py:130
  52.8 0.6 collective-permute-start.5
  53.4 0.0 collective-permute-done.4.refs_1_
  53.5 0.8 %shard_map.73 = (bf16[256,1024]{1,0:T(8,128)(2,1)S(1)}, bf16[256,1024]{1,0:T(8,128)(2,1)S(1)}) custom-call(f32[1,1]{1,0:T(1,128)} %bitcast.16.spread_ref, f32[256,128]{1,0:T(8,128)S(1)} %get-tuple-element.16.aimed_ref, f32[512,128]{1,0:T(8,128)S(1)} %bitcast.27, f32[512,128]{1,0:T(8,128)S(1)} %collective-permute-done.4.refs_1_), custom_call_target="tpu_custom_call" | custom-call | flops 402653184 | bytes 655364 | tf_op jit(solution)/shard_map/pallas_call | solution.py:130
  54.3 0.3 collective-permute-done.5.refs_1_
  54.6 1.2 %shard_map.75 = f32[8,64,128]{2,1,0:T(8,128)} custom-call(bf16[256,1024]{1,0:T(8,128)(2,1)S(1)} %get-tuple-element.8.high_ref, bf16[256,1024]{1,0:T(8,128)(2,1)S(1)} %get-tuple-element.9.low_ref, f32[512,128]{1,0:T(8,128)S(1)} %shard_map.74.refs_0_, f32[512,128]{1,0:T(8,128)S(1)} %collective-permute-done.5.refs_1_, f32[256,128]{1,0:T(8,128)S(1)} %get-tuple-element.15.refs_2_), custom_call_target="tpu_custom_call" | custom-call | flops 268435456 | bytes 2752512 | tf_op jit(solution)/shard_map/pallas_call | solution.py:130
  55.7 3.4 %all-to-all-start.3 = ((f32[8,64,128]{2,1,0:T(8,128)}), f32[8,64,128]{2,1,0:T(8,128)S(1)}, u32[]{:S(2)}, u32[]{:S(2)}) async-start(f32[8,64,128]{2,1,0:T(8,128)} %shard_map.75), calls=%async_computation.3 | async-start | bytes 524288 | tf_op jit(solution)/shard_map/all_to_all | solution.py:208
  59.2 1.5 %shard_map.76 = f32[32,128]{1,0:T(8,128)S(1)} custom-call(f32[1,1]{1,0:T(1,128)} %bitcast.17.spread_ref, f32[32,128]{1,0:T(8,128)S(1)} %multiply_add_fusion.own_ref, f32[512,128]{1,0:T(8,128)S(1)} %bitcast.28, f32[512,128]{1,0:T(8,128)S(1)} %collective-permute-done.4.refs_1_), custom_call_target="tpu_custom_call" | custom-call | flops 33554432 | bytes 540676 | tf_op jit(solution)/shard_map/pallas_call | solution.py:130
  60.7 8.2 %all-to-all-done.3 = f32[8,64,128]{2,1,0:T(8,128)S(1)} async-done(((f32[8,64,128]{2,1,0:T(8,128)}), f32[8,64,128]{2,1,0:T(8,128)S(1)}, u32[]{:S(2)}, u32[]{:S(2)}) %all-to-all-start.3) | async-done | bytes 262176 | tf_op jit(solution)/shard_map/all_to_all | solution.py:208
  68.9 0.6 slice_subtract_fusion
  (11 shorter events, 0.2 us)
Async XLA Ops:
  0.6 10.1 %copy-start = (f32[2048,128]{1,0:T(8,128)S(1)}, f32[2048,128]{1,0:T(8,128)}, u32[]{:S(2)}) copy-start(f32[2048,128]{1,0:T(8,128)} %param.7) | copy-start | bytes 3145732
  0.6 0.8 %copy-start.1 = (f32[32,128]{1,0:T(8,128)S(1)}, f32[32,128]{1,0:T(8,128)}, u32[]{:S(2)}) copy-start(f32[32,128]{1,0:T(8,128)} %x_ref.1) | copy-start | bytes 49156
  2.2 8.5 %copy-start.2 = (s32[512]{0:T(512)S(1)}, s32[512]{0:T(512)}, u32[]{:S(2)}) copy-start(s32[512]{0:T(512)} %param.9) | copy-start | bytes 6148
  2.2 18.4 %all-to-all-start = ((f32[16,32,128]{2,1,0:T(8,128)}), f32[16,32,128]{2,1,0:T(8,128)S(1)}, u32[]{:S(2)}, u32[]{:S(2)}) async-start(f32[16,32,128]{2,1,0:T(8,128)} %shard_map.68), calls=%async_computation | async-start | bytes 524288 | tf_op jit(solution)/shard_map/all_to_all | solution.py:180
  10.7 1.1 %copy-start.3 = (s32[2048]{0:T(1024)S(1)}, s32[2048]{0:T(1024)}, u32[]{:S(2)}) copy-start(s32[2048]{0:T(1024)} %param.8) | copy-start | bytes 24580
  11.8 8.8 %collective-permute-start.1 = (f32[512,128]{1,0:T(8,128)S(1)}, f32[512,128]{1,0:T(8,128)S(1)}, u32[]{:S(2)}, u32[]{:S(2)}) collective-permute-start(f32[512,128]{1,0:T(8,128)S(1)} %gather_fusion), channel_id=1, source_target_pairs={{0,1},{1,0},{2,3},{3,2},{4,5},{5,4},{6,7},{7,6},{8,9},{9,8},{10,11... | collective-permute-start | bytes 786440 | tf_op jit(solution)/shard_map/ppermute | solution.py:145
  12.1 8.4 %collective-permute-start.2 = (f32[1,512]{1,0:T(1,128)S(1)}, f32[1,512]{1,0:T(1,128)S(1)}, u32[]{:S(2)}, u32[]{:S(2)}) collective-permute-start(f32[1,512]{1,0:T(1,128)S(1)} %bitcast.29), channel_id=1, source_target_pairs={{0,1},{1,0},{2,3},{3,2},{4,5},{5,4},{6,7},{7,6},{8,9},{9,8},{10,11... | collective-permute-start | bytes 6152 | tf_op jit(solution)/shard_map/ppermute | solution.py:145
  20.5 1.7 %collective-permute-start = (f32[512,128]{1,0:T(8,128)S(1)}, f32[512,128]{1,0:T(8,128)S(1)}, u32[]{:S(2)}, u32[]{:S(2)}) collective-permute-start(f32[512,128]{1,0:T(8,128)S(1)} %bitcast.18), channel_id=1, source_target_pairs={{0,1},{1,0},{2,3},{3,2},{4,5},{5,4},{6,7},{7,6},{8,9},{9,8},{10,11... | collective-permute-start | bytes 786440 | tf_op jit(solution)/shard_map/ppermute | solution.py:145
  21.6 1.6 %collective-permute-start.3 = (f32[256,128]{1,0:T(8,128)S(1)}, f32[256,128]{1,0:T(8,128)S(1)}, u32[]{:S(2)}, u32[]{:S(2)}) collective-permute-start(f32[256,128]{1,0:T(8,128)S(1)} %shard_map.70.refs_0_), channel_id=1, source_target_pairs={{0,1},{1,0},{2,3},{3,2},{4,5},{5,4},{6,7},{7,6},{8,9},{9,8},{10,11... | collective-permute-start | bytes 393224 | tf_op jit(solution)/shard_map/ppermute | solution.py:145
  24.4 14.2 %all-to-all-start.1 = ((f32[16,32,128]{2,1,0:T(8,128)}), f32[16,32,128]{2,1,0:T(8,128)S(1)}, u32[]{:S(2)}, u32[]{:S(2)}) async-start(f32[16,32,128]{2,1,0:T(8,128)} %bitcast.5), calls=%async_computation.1 | async-start | bytes 524288 | tf_op jit(solution)/shard_map/all_to_all | solution.py:208
  51.2 2.2 %collective-permute-start.4 = (f32[512,128]{1,0:T(8,128)S(1)}, f32[512,128]{1,0:T(8,128)S(1)}, u32[]{:S(2)}, u32[]{:S(2)}) collective-permute-start(f32[512,128]{1,0:T(8,128)S(1)} %bitcast.24), channel_id=1, source_target_pairs={{0,1},{1,0},{2,3},{3,2},{4,5},{5,4},{6,7},{7,6},{8,9},{9,8},{10,11... | collective-permute-start | bytes 786440 | tf_op jit(solution)/shard_map/ppermute | solution.py:145
  52.8 1.7 %collective-permute-start.5 = (f32[512,128]{1,0:T(8,128)S(1)}, f32[512,128]{1,0:T(8,128)S(1)}, u32[]{:S(2)}, u32[]{:S(2)}) collective-permute-start(f32[512,128]{1,0:T(8,128)S(1)} %shard_map.74.refs_0_), channel_id=1, source_target_pairs={{0,1},{1,0},{2,3},{3,2},{4,5},{5,4},{6,7},{7,6},{8,9},{9,8},{10,11... | collective-permute-start | bytes 786440 | tf_op jit(solution)/shard_map/ppermute | solution.py:145
  55.7 13.1 %all-to-all-start.3 = ((f32[8,64,128]{2,1,0:T(8,128)}), f32[8,64,128]{2,1,0:T(8,128)S(1)}, u32[]{:S(2)}, u32[]{:S(2)}) async-start(f32[8,64,128]{2,1,0:T(8,128)} %shard_map.75), calls=%async_computation.3 | async-start | bytes 524288 | tf_op jit(solution)/shard_map/all_to_all | solution.py:208

commit v4 on v3

--- a/solution.py
+++ b/solution.py
@@ -85,41 +85,34 @@
     return with_sources
 
 
-def weights_kernel(spread_ref, aimed_ref, *refs):
-    source_refs, (high_ref, low_ref) = refs[:-2], refs[-2:]
-    with_sources = kernel_of(aimed_ref[...], 1.0 / spread_ref[...])
-    start = 0
+def weights_kernel(inverse_ref, aimed_ref, own_ref, *refs):
+    source_refs, (high_ref, low_ref, extra_ref) = refs[:-3], refs[-3:]
+    inverse = inverse_ref[...]
+    own, count = own_ref[...], aimed_ref.shape[0]
+    with_sources = kernel_of(jnp.concatenate([aimed_ref[...], own], axis=0), inverse)
+    start, cubes, pulled = 0, None, None
     for source in chunks(source_refs, SOURCE_CHUNK):
         span = slice(start, start + source.shape[0])
-        high_ref[:, span], low_ref[:, span] = parts(with_sources(source)[0], 2)
         start += source.shape[0]
-
-
-def drive_kernel(local, high_ref, low_ref, *refs):
+        kernel, pulls = with_sources(source)
+        high_ref[:, span], low_ref[:, span] = parts(kernel[:count], 2)
+        mine = kernel[count:]
+        cubed = mine * mine * mine
+        pull = dot(jnp.concatenate(parts(mine + cubed * inverse, 2), axis=0), pulls)
+        cube = jnp.sum(cubed, axis=1, keepdims=True)
+        cubes, pulled = (cube, pull) if cubes is None else (cubes + cube, pulled + pull)
+    pulled = folded(pulled)
+    extra_ref[...] = own * (cubes * inverse) - (pulled[:own.shape[0]] + pulled[own.shape[0]:])
+
+
+def drive_kernel(local, riding, high_ref, low_ref, *refs):
     grad_refs, riders, out_ref = refs[:2], refs[2:-1], refs[-1]
     grads = jnp.concatenate([lanes(*parts(ref[...], 2)) for ref in grad_refs], axis=0)
     drive = folded(dot(high_ref[...], grads) + dot(low_ref[...], grads))
-    if not riders:
-        out_ref[...] = drive
-        return
     for j in range(out_ref.shape[0]):
         out_ref[j, :local, :] = drive[j * local:(j + 1) * local, :]
-        out_ref[j, local:, :] = riders[0][j * local:(j + 1) * local, :]
-
-
-def own_kernel(spread_ref, own_ref, *refs):
-    source_refs, out_ref = refs[:-1], refs[-1]
-    inverse = 1.0 / spread_ref[...]
-    own = own_ref[...]
-    with_sources = kernel_of(own, inverse)
-    cubes, pulled = None, None
-    for source in chunks(source_refs, SOURCE_CHUNK):
-        kernel, pulls = with_sources(source)
-        cubed = kernel * kernel * kernel
-        high, low = parts(kernel + cubed * inverse, 2)
-        cube, pull = jnp.sum(cubed, axis=1, keepdims=True), dot(high, pulls) + dot(low, pulls)
-        cubes, pulled = (cube, pull) if cubes is None else (cubes + cube, pulled + pull)
-    out_ref[...] = own * (cubes * inverse) - folded(pulled)
+        if riding:
+            out_ref[j, local:, :] = riders[0][j * local:(j + 1) * local, :]
 
 
 VMEM_SPEC = pl.BlockSpec(memory_space=pltpu.VMEM)
@@ -161,13 +154,13 @@
     factor = STEP_SIZE / (local * doms * chips * cores)
     dom, chip = lax.axis_index("dom"), lax.axis_index("chip")
     everywhere = ("dom", "chip")
-    spread = length_scale.reshape(1, 1)
 
     rows = features[batch_index]
     targets = picked(labels, batch_index)
     pair_targets = swapped(targets)
     targets = jnp.concatenate([targets, pair_targets], axis=1)
     row_sets = (rows, swapped(rows), targets)
+    inverse = (1.0 / length_scale).reshape(1, 1)
     data = rows.shape[0] * cores
 
     current = positions
@@ -178,39 +171,28 @@
         else:
             tiled = jnp.broadcast_to(current[None], (doms * chips, local, width))
         mine = lax.all_to_all(tiled, everywhere, 0, 0, tiled=True).reshape(-1, width)
-        own_block = lax.dynamic_slice_in_dim(mine, dom * block, block, 0)
+        pair = swapped(mine)
+        aimed = lax.dynamic_slice_in_dim(mine, dom * block, block, 0)
         if iteration == 0:
-            current = lax.dynamic_slice_in_dim(own_block, chip * local, local, 0)
-        pair = swapped(mine)
-        if last:
-            aimed, graded, sources = own_block, mine, (mine, pair)
-        else:
-            pair_block = lax.dynamic_slice_in_dim(pair, dom * block, block, 0)
-            aimed, graded, sources = mine, own_block, (own_block, pair_block)
-        count, found = aimed.shape[0], sum(s.shape[0] for s in sources)
+            current = lax.dynamic_slice_in_dim(mine, dom * block + chip * local, local, 0)
+        found = mine.shape[0] * cores
         grads = run(
-            functools.partial(grad_kernel, scale), array(graded.shape[0], width), graded, *row_sets,
-            flops=16 * graded.shape[0] * data * width,
+            functools.partial(grad_kernel, scale), array(*mine.shape), mine, *row_sets,
+            flops=16 * mine.shape[0] * data * width,
         )
         pair_grads = swapped(grads)
-        high, low = run(
-            weights_kernel, (array(count, found, dtype=BF16),) * 2, spread, aimed, *sources,
-            flops=12 * count * found * width,
+        part = array(block, found, dtype=BF16)
+        high, low, extra = run(
+            weights_kernel, (part, part, array(local, width)), inverse, aimed, current, mine, pair,
+            flops=12 * (block + local) * found * width,
         )
-        drive = functools.partial(drive_kernel, local)
-        flops = 8 * count * found * width
-        if last:
-            rider = lax.dynamic_slice_in_dim(grads, dom * block, block, 0)
-            shape = array(chips, 2 * local, width)
-            moves = run(drive, shape, high, low, grads, pair_grads, rider, flops=flops)
-        else:
-            moves = run(drive, array(count, width), high, low, grads, pair_grads, flops=flops)
-        moves = lax.all_to_all(
-            moves.reshape(-1, moves.shape[-2] if last else local, width),
-            "chip" if last else everywhere, 0, 0, tiled=True,
+        riders = [lax.dynamic_slice_in_dim(grads, dom * block, block, 0)] if last else []
+        moves = run(
+            functools.partial(drive_kernel, local, last),
+            array(chips, (2 if last else 1) * local, width), high, low, grads, pair_grads, *riders,
+            flops=8 * block * found * width,
         )
-        extra = run(own_kernel, array(local, width), spread, current, mine, pair, flops=flops // chips)
-        result = jnp.sum(moves, axis=0)
+        result = jnp.sum(lax.all_to_all(moves, "chip", 0, 0, tiled=True), axis=0)
         if last:
             score = result[local:] - current
         current = current + factor * (result[:local] + extra)

time: 70 us -> 65.1 us (0.930)
  blocking collectives: 12.6 us -> 34.9 us
  waiting for transfers between devices: 25 us -> 7.19 us
  starting transfers between devices: 17.2 us -> 10.2 us
  Pallas kernels: 10.3 us -> 7.97 us
    all_to_all x0 -> x2, blocking collectives: none -> 22.6 us  [shards(): result = jnp.sum(lax.all_to_all(moves, 'chip', 0, 0, tiled=True), axis=0)]
    all_to_all x2 -> x0, waiting for transfers between devices: 17.3 us -> none  [shards(): lax.all_to_all(moves.reshape(-1, moves.shape[-2] if last else local, widt...]
    all_to_all x2 -> x0, starting transfers between devices: 6.94 us -> none  [shards(): lax.all_to_all(moves.reshape(-1, moves.shape[-2] if last else local, widt...]
    pallas_call x9 -> x7, Pallas kernels: 10.3 us -> 7.97 us  [run(): pl.pallas_call(kernel, out_shape=out_shape, in_specs=[VMEM_SPEC] * len(ar...]
  transfers between devices with their start and end apart: 9 -> 7, of which waited for: 5 -> 2; matrix products, arithmetic and copies ran while one was open for 2% -> 2% of each run, Pallas kernels for 10% -> 10%
where the time goes in v4:
time: 65.1 us; the launch traced here: 64.7 us
  blocking collectives  34.9 us (54%)
  starting transfers between devices  10.2 us (16%)
  Pallas kernels  7.97 us (12%)
  waiting for transfers between devices  7.19 us (11%)
  local copies, waits for them, and re-layouts  1.9 us (3%)
  between operations  1.51 us (2%)
  other arithmetic  0.68 us (1%)
    all_to_all x2, blocking collectives, shards(): result = jnp.sum(lax.all_to_all(moves, 'chip', 0, 0, tiled=True), axis=0)  22.6 us
    all_to_all x1, blocking collectives, shards(): lax.all_to_all(tiled, everywhere, 0, 0, tiled=True).reshape(-1, width)  12.4 us
    all_to_all x1, starting transfers between devices, shards(): lax.all_to_all(tiled, everywhere, 0, 0, tiled=True).reshape(-1, width)  8.47 us
    pallas_call x7, Pallas kernels, run(): pl.pallas_call(kernel, out_shape=out_shape, in_specs=[VMEM_SPEC] * len(ar...  7.97 us
    all_to_all x1, waiting for transfers between devices, shards(): lax.all_to_all(tiled, everywhere, 0, 0, tiled=True).reshape(-1, width)  7.05 us
    ppermute x6, starting transfers between devices, swapped(): return lax.ppermute(x, 'core', [(0, 1), (1, 0)])  1.77 us
  transfers between devices with their start and end apart: 7, of which 2 were waited for; matrix products, arithmetic and copies ran while one was open for 2% of the time, Pallas kernels for 10%

profile of v4, /device:TPU:0, one launch (start us, length us, event | category | flops | bytes accessed | tf_op | source)
XLA Modules:
  0.0 64.7 jit_solution(1806602755090963746)
XLA Ops:
  0.6 0.0 copy-start
  0.6 0.0 copy-start.1
  0.7 0.8 %copy-done.1 = f32[32,128]{1,0:T(8,128)S(1)} copy-done((f32[32,128]{1,0:T(8,128)S(1)}, f32[32,128]{1,0:T(8,128)}, u32[]{:S(2)}) %copy-start.1) | copy-done | bytes 16408
  1.5 0.7 %shard_map.68 = f32[16,32,128]{2,1,0:T(8,128)} custom-call(f32[32,128]{1,0:T(8,128)S(1)} %copy-done.1), custom_call_target="tpu_custom_call" | custom-call | bytes 16384 | tf_op jit(solution)/shard_map/pallas_call | solution.py:123
  2.2 0.0 copy-start.2
  2.2 8.5 %all-to-all-start = ((f32[16,32,128]{2,1,0:T(8,128)}), f32[16,32,128]{2,1,0:T(8,128)S(1)}, u32[]{:S(2)}, u32[]{:S(2)}) async-start(f32[16,32,128]{2,1,0:T(8,128)} %shard_map.68), calls=%async_computation | async-start | bytes 524288 | tf_op jit(solution)/shard_map/all_to_all | solution.py:173
  10.7 0.0 copy-done.2
  10.7 0.0 copy-done
  10.7 0.0 copy-start.3
  10.7 1.0 %gather_fusion = f32[512,128]{1,0:T(8,128)S(1)} fusion(f32[2048,128]{1,0:T(8,128)S(1)} %copy-done, s32[1024]{0:T(1024)S(1)} %pad_clamp_fusion), kind=kCustom, calls=%fused_computation | custom fusion | bytes 526336 | tf_op jit(solution)/shard_map/gather | solution.py:158
  11.8 0.1 collective-permute-start.1
  11.8 0.0 copy-done.3
  11.8 0.2 fusion.1
  12.1 0.6 collective-permute-start.2
  13.3 0.1 collective-permute-done.2
  13.5 7.1 %all-to-all-done = f32[16,32,128]{2,1,0:T(8,128)S(1)} async-done(((f32[16,32,128]{2,1,0:T(8,128)}), f32[16,32,128]{2,1,0:T(8,128)S(1)}, u32[]{:S(2)}, u32[]{:S(2)}) %all-to-all-start) | async-done | bytes 262176 | tf_op jit(solution)/shard_map/all_to_all | solution.py:173
  20.5 0.0 collective-permute-start
  20.5 0.0 collective-permute-done.1.rows_b_ref
  20.5 1.6 %shard_map.70.refs_0_ = f32[512,128]{1,0:T(8,128)S(1)} custom-call(f32[512,128]{1,0:T(8,128)S(1)} %bitcast.14, f32[512,128]{1,0:T(8,128)S(1)} %gather_fusion, f32[512,128]{1,0:T(8,128)S(1)} %collective-permute-done.1.rows_b_ref, f32[1,1024]{1,0:T(1,128)S(1)} %pad_maximum_fusion.targets_ref), custom_call_target="tpu_custom_call" | custom-call | flops 1073741824 | bytes 790528 | tf_op jit(solution)/shard_map/pallas_call | solution.py:123
  22.1 0.6 collective-permute-start.3
  22.7 0.0 collective-permute-done.refs_1_
  22.7 1.6 %shard_map.69 = (bf16[256,1024]{1,0:T(8,128)(2,1)S(1)}, bf16[256,1024]{1,0:T(8,128)(2,1)S(1)}, f32[32,128]{1,0:T(8,128)S(1)}) custom-call(f32[1,1]{1,0:T(1,128)} %bitcast.1.inverse_ref, f32[256,128]{1,0:T(8,128)S(1)} %constant_dynamic-slice_fusion.2.aimed_ref, f32[32,128]{1,0:T(8,128)S(1)} %constant_dynamic-slice_fusion.3.own_ref, f32[512,128]{1,0:T(8,128)S(1)} %bitcast.17, ...), custom_call_target="tpu_custom_call" | custom-call | flops 452984832 | bytes 671748 | tf_op jit(solution)/shard_map/pallas_call | solution.py:123
  24.3 0.0 collective-permute-done.3.refs_1_
  24.3 0.5 shard_map.71
  24.8 10.4 %all_to_all.20 = f32[8,32,128]{2,1,0:T(8,128)S(1)} all-to-all(f32[8,32,128]{2,1,0:T(8,128)S(1)} %shard_map.71), channel_id=1, replica_groups=mesh['dom'=2,'chip'=8,'core'=2] {'chip'}, dimensions={0} | all-to-all | bytes 262144 | tf_op jit(solution)/shard_map/all_to_all | solution.py:195
  35.3 12.4 %all_to_all.21 = f32[16,32,128]{2,1,0:T(8,128)S(1)} all-to-all(f32[16,32,128]{2,1,0:T(8,128)S(1)} %broadcast_in_dim.21), channel_id=1, replica_groups=mesh['dom'=2,'chip'=8,'core'=2] {'dom','chip'}, dimensions={0} | all-to-all | bytes 524288 | tf_op jit(solution)/shard_map/all_to_all | solution.py:173
  47.6 0.0 collective-permute-start.4
  47.6 1.6 %shard_map.73.refs_0_ = f32[512,128]{1,0:T(8,128)S(1)} custom-call(f32[512,128]{1,0:T(8,128)S(1)} %bitcast.20, f32[512,128]{1,0:T(8,128)S(1)} %gather_fusion, f32[512,128]{1,0:T(8,128)S(1)} %collective-permute-done.1.rows_b_ref, f32[1,1024]{1,0:T(1,128)S(1)} %pad_maximum_fusion.targets_ref), custom_call_target="tpu_custom_call" | custom-call | flops 1073741824 | bytes 790528 | tf_op jit(solution)/shard_map/pallas_call | solution.py:123
  49.2 0.6 collective-permute-start.5
  49.8 0.0 collective-permute-done.4.refs_1_
  49.8 1.6 %shard_map.72 = (bf16[256,1024]{1,0:T(8,128)(2,1)S(1)}, bf16[256,1024]{1,0:T(8,128)(2,1)S(1)}, f32[32,128]{1,0:T(8,128)S(1)}) custom-call(f32[1,1]{1,0:T(1,128)} %bitcast.1.inverse_ref, f32[256,128]{1,0:T(8,128)S(1)} %get-tuple-element.20.aimed_ref, f32[32,128]{1,0:T(8,128)S(1)} %multiply_add_fusion.own_ref, f32[512,128]{1,0:T(8,128)S(1)} %bitcast.22, ...), custom_call_target="tpu_custom_call" | custom-call | flops 452984832 | bytes 671748 | tf_op jit(solution)/shard_map/pallas_call | solution.py:123
  51.4 0.0 collective-permute-done.5.refs_1_
  51.4 0.4 shard_map.74
  51.9 12.2 %all_to_all.22 = f32[8,64,128]{2,1,0:T(8,128)S(1)} all-to-all(f32[8,64,128]{2,1,0:T(8,128)S(1)} %shard_map.74), channel_id=1, replica_groups=mesh['dom'=2,'chip'=8,'core'=2] {'chip'}, dimensions={0} | all-to-all | bytes 524288 | tf_op jit(solution)/shard_map/all_to_all | solution.py:195
  64.1 0.6 slice_subtract_fusion
  (10 shorter events, 0.1 us)
Async XLA Ops:
  0.6 10.1 %copy-start = (f32[2048,128]{1,0:T(8,128)S(1)}, f32[2048,128]{1,0:T(8,128)}, u32[]{:S(2)}) copy-start(f32[2048,128]{1,0:T(8,128)} %param.7) | copy-start | bytes 3145732
  0.6 0.8 %copy-start.1 = (f32[32,128]{1,0:T(8,128)S(1)}, f32[32,128]{1,0:T(8,128)}, u32[]{:S(2)}) copy-start(f32[32,128]{1,0:T(8,128)} %x_ref.1) | copy-start | bytes 49156
  2.2 8.5 %copy-start.2 = (s32[512]{0:T(512)S(1)}, s32[512]{0:T(512)}, u32[]{:S(2)}) copy-start(s32[512]{0:T(512)} %param.9) | copy-start | bytes 6148
  2.2 18.4 %all-to-all-start = ((f32[16,32,128]{2,1,0:T(8,128)}), f32[16,32,128]{2,1,0:T(8,128)S(1)}, u32[]{:S(2)}, u32[]{:S(2)}) async-start(f32[16,32,128]{2,1,0:T(8,128)} %shard_map.68), calls=%async_computation | async-start | bytes 524288 | tf_op jit(solution)/shard_map/all_to_all | solution.py:173
  10.7 1.1 %copy-start.3 = (s32[2048]{0:T(1024)S(1)}, s32[2048]{0:T(1024)}, u32[]{:S(2)}) copy-start(s32[2048]{0:T(1024)} %param.8) | copy-start | bytes 24580
  11.8 8.8 %collective-permute-start.1 = (f32[512,128]{1,0:T(8,128)S(1)}, f32[512,128]{1,0:T(8,128)S(1)}, u32[]{:S(2)}, u32[]{:S(2)}) collective-permute-start(f32[512,128]{1,0:T(8,128)S(1)} %gather_fusion), channel_id=1, source_target_pairs={{0,1},{1,0},{2,3},{3,2},{4,5},{5,4},{6,7},{7,6},{8,9},{9,8},{10,11... | collective-permute-start | bytes 786440 | tf_op jit(solution)/shard_map/ppermute | solution.py:138
  12.1 1.4 %collective-permute-start.2 = (f32[1,512]{1,0:T(1,128)S(1)}, f32[1,512]{1,0:T(1,128)S(1)}, u32[]{:S(2)}, u32[]{:S(2)}) collective-permute-start(f32[1,512]{1,0:T(1,128)S(1)} %bitcast.23), channel_id=1, source_target_pairs={{0,1},{1,0},{2,3},{3,2},{4,5},{5,4},{6,7},{7,6},{8,9},{9,8},{10,11... | collective-permute-start | bytes 6152 | tf_op jit(solution)/shard_map/ppermute | solution.py:138
  20.5 2.2 %collective-permute-start = (f32[512,128]{1,0:T(8,128)S(1)}, f32[512,128]{1,0:T(8,128)S(1)}, u32[]{:S(2)}, u32[]{:S(2)}) collective-permute-start(f32[512,128]{1,0:T(8,128)S(1)} %bitcast.13), channel_id=1, source_target_pairs={{0,1},{1,0},{2,3},{3,2},{4,5},{5,4},{6,7},{7,6},{8,9},{9,8},{10,11... | collective-permute-start | bytes 786440 | tf_op jit(solution)/shard_map/ppermute | solution.py:138
  22.1 2.2 %collective-permute-start.3 = (f32[512,128]{1,0:T(8,128)S(1)}, f32[512,128]{1,0:T(8,128)S(1)}, u32[]{:S(2)}, u32[]{:S(2)}) collective-permute-start(f32[512,128]{1,0:T(8,128)S(1)} %shard_map.70.refs_0_), channel_id=1, source_target_pairs={{0,1},{1,0},{2,3},{3,2},{4,5},{5,4},{6,7},{7,6},{8,9},{9,8},{10,11... | collective-permute-start | bytes 786440 | tf_op jit(solution)/shard_map/ppermute | solution.py:138
  47.6 2.2 %collective-permute-start.4 = (f32[512,128]{1,0:T(8,128)S(1)}, f32[512,128]{1,0:T(8,128)S(1)}, u32[]{:S(2)}, u32[]{:S(2)}) collective-permute-start(f32[512,128]{1,0:T(8,128)S(1)} %bitcast.19), channel_id=1, source_target_pairs={{0,1},{1,0},{2,3},{3,2},{4,5},{5,4},{6,7},{7,6},{8,9},{9,8},{10,11... | collective-permute-start | bytes 786440 | tf_op jit(solution)/shard_map/ppermute | solution.py:138
  49.2 2.2 %collective-permute-start.5 = (f32[512,128]{1,0:T(8,128)S(1)}, f32[512,128]{1,0:T(8,128)S(1)}, u32[]{:S(2)}, u32[]{:S(2)}) collective-permute-start(f32[512,128]{1,0:T(8,128)S(1)} %shard_map.73.refs_0_), channel_id=1, source_target_pairs={{0,1},{1,0},{2,3},{3,2},{4,5},{5,4},{6,7},{7,6},{8,9},{9,8},{10,11... | collective-permute-start | bytes 786440 | tf_op jit(solution)/shard_map/ppermute | solution.py:138
